TPU v7x, 1024 devices: a whole 8x8x8 slice. The times are simulated.
1024 devices in a mesh: space: 8 (over x_hi, core), modes: 128 (over z, x_lo, y).
Axes of the slice: x: 8 (x_hi: 4, x_lo: 2; x = x_hi * 2 + x_lo), y: 8, z: 8, core: 2. Of those that a mesh axis runs over, the one named last changes fastest.
Arguments:
- modes_field: float32 [24576, 256], P('space', 'modes'), may hold values from -6 to 6
- slopes: float32 [24576, 256], P('space', 'modes'), may hold values from -6 to 6
Outputs:
- tensor: float32 [256, 256, 256], P('space', 'modes')
All inputs are finite; a program needn't handle non-finite values.
Results may differ from a plain program's by a relative error of at most 0.0001.
Values sent between devices are 32-bit elements; how exact they have to be, the bound alone decides.
No kernel may reach another device: no remote copies, remote signals or barrier semaphores. Data moves between devices by JAX's collectives and lax.ppermute only.
A program may use at most 32 MiB of HBM per device.

v0:
```python
import math

import jax
import jax.numpy as jnp
from jax import lax
from jax.sharding import PartitionSpec as P


def project(panel, weighted):
    return lax.dot_general(
        panel,
        weighted,
        (((0,), (0,)), ((), ())),
        precision=lax.Precision.HIGHEST,
        preferred_element_type=jnp.float32,
    )


def per_device(modes_field, slopes):
    row_count = modes_field.shape[0]
    own_modes = modes_field.shape[1]
    factor = 1.0 / math.sqrt(row_count * lax.axis_size("space"))
    slope_all = lax.all_gather(slopes, "modes", axis=1, tiled=True)
    width = slope_all.shape[1]
    weighted = (modes_field[:, :, None] * slope_all[:, None, :] * factor).reshape(
        row_count, own_modes * width
    )
    partial_tensor = project(lax.all_gather(modes_field, "modes", axis=1, tiled=True), weighted)
    summed = lax.psum_scatter(partial_tensor, "space", scatter_dimension=0, tiled=True)
    return summed.reshape(summed.shape[0], own_modes, width)


def solution(mesh):
    placed = (P("space", "modes"), P("space", "modes"))
    return jax.shard_map(
        per_device, mesh=mesh, in_specs=placed, out_specs=P("space", "modes", None), check_vma=False
    )
```

profile of v0, /device:TPU:4, one launch (start us, length us, event | category | flops | bytes accessed | tf_op | source)
XLA Modules:
  0.0 1265.8 jit_solution(8079365382570628143)
XLA Ops:
  6.5 0.0 all-gather.5.cloned.1.call-start
  6.5 0.7 all-gather.5.cloned.1.call-update
  7.3 0.0 all-gather.7.cloned.1.call-start
  7.3 0.7 all-gather.7.cloned.1.call-update
  8.0 0.0 reduce-scatter.4.cloned.1.call-start
  8.1 2.4 copy.6
  10.5 605.8 %all-gather.5.cloned.1.call-done = f32[128,2,3072]{2,1,0:T(2,128)} async-done(((f32[1,2,3072]{2,1,0:T(2,128)}), f32[128,2,3072]{2,1,0:T(2,128)}) %all-gather.5.cloned.1.call-update) | async-done | bytes 3145744 | tf_op jit(solution)/shard_map/all_gather | solution.py:23
  616.3 3.9 reshape.13
  620.2 2.4 copy.7
  622.5 10.4 multiply_multiply_fusion
  633.0 3.4 copy.11
  636.3 570.4 %all-gather.7.cloned.1.call-done = f32[128,2,3072]{2,1,0:T(2,128)} async-done(((f32[1,2,3072]{2,1,0:T(2,128)}), f32[128,2,3072]{2,1,0:T(2,128)}) %all-gather.7.cloned.1.call-update) | async-done | bytes 3145744 | tf_op jit(solution)/shard_map/all_gather | solution.py:28
  1206.7 3.9 reshape.15
  1210.6 12.8 %convolution_bitcast_fusion = f32[256,512]{0,1:T(8,128)} fusion(f32[3072,512]{1,0:T(8,128)} %bitcast.15, f32[256,3072]{1,0:T(8,128)S(1)} %reshape.15), kind=kOutput, calls=%fused_computation.1 | convolution fusion | flops 4831838208 | bytes 9961472 | tf_op jit(solution)/shard_map/dot_general | solution.py:10
  1223.4 2.0 copy.9
  1225.4 0.0 reduce-scatter.4.cloned.1.call-update
  1225.5 32.1 %reduce-scatter.4.cloned.1.call-done = f32[32,512]{1,0:T(8,128)} async-done(((f32[256,512]{1,0:T(8,128)}), f32[32,512]{1,0:T(8,128)}) %reduce-scatter.4.cloned.1.call-update) | async-done | bytes 65552
  1257.6 1.0 copy.10
  1258.5 0.7 copy.8
Async XLA Ops:
  6.5 609.7 %all-gather.5.cloned.1.call-start = ((), (), s32[]{:S(2)}) async-start(), calls=%async_computation.1 | async-start | bytes 3170304 | tf_op jit(solution)/shard_map/all_gather | solution.py:23
  7.3 1199.4 %all-gather.7.cloned.1.call-start = ((), (), s32[]{:S(2)}) async-start(), calls=%async_computation.2 | async-start | bytes 3170304 | tf_op jit(solution)/shard_map/all_gather | solution.py:28
  8.0 1249.6 %reduce-scatter.4.cloned.1.call-start = ((), (), s32[]{:S(2)}) async-start(), calls=%async_computation.3 | async-start | bytes 589824
Sparse Core Ops, SparseCore 0:
  10.0 606.2 all-gather.4
  618.9 587.7 all-gather.6
  1225.6 31.9 reduce-scatter.3
where the time goes:
time: 1270 us
  waiting for transfers between devices  1210 us (95%)
  local copies, waits for them, and re-layouts  19.6 us (2%)
  between operations  13.1 us (1%)
  matrix products  12.8 us (1%)
    all_gather x1, waiting for transfers between devices, per_device(): slope_all = lax.all_gather(slopes, 'modes', axis=1, tiled=True)  606 us
    all_gather x1, waiting for transfers between devices, per_device(): lax.all_gather(modes_field, 'modes', axis=1, tiled=True)  570 us
    unnamed x4, waiting for transfers between devices  33.5 us
  transfers between devices with their start and end apart: 3, of which 3 were waited for; matrix products, arithmetic and copies ran while one was open for 2% of the time, Pallas kernels for 0%

commit v1 on v0

v1 whole, which is shorter than its diff:
```python
import functools
import math

import jax
import jax.numpy as jnp
from jax import lax
from jax.experimental import pallas as pl
from jax.experimental.pallas import tpu as pltpu
from jax.sharding import Mesh
from jax.sharding import PartitionSpec as P

AXES = ("xh", "core", "z", "xl", "yh", "yl")
SPACE = ("xh", "core")
MODES = ("z", "xl", "yh", "yl")
VMEM = pl.BlockSpec(memory_space=pltpu.VMEM)
SMEM = pl.BlockSpec(memory_space=pltpu.SMEM)


def spread_kernel(m_ref, s_ref, out_ref):
    rows = out_ref.shape[3]
    for half in range(2):
        cut = slice(half * rows, (half + 1) * rows)
        for y in range(8):
            out_ref[half, y, 0:2, :] = m_ref[:, cut]
            out_ref[half, y, 2:4, :] = s_ref[:, cut]


def pick_kernel(at_ref, near_ref, out_ref):
    yh, yl = at_ref[1], at_ref[2]
    for shard in range(5):
        y = 2 * shard + yl if shard < 4 else 2 * yh + 1 - yl
        for xl in range(2):
            piece = near_ref[xl, y, 0:2, :]
            for z in range(8):
                out_ref[z, shard, 2 * xl : 2 * xl + 2, :] = piece


def tensor_kernel(at_ref, near_ref, far_ref, keep_ref, send_ref, left, left2, mode_j, slope, prod_hi, prod_lo):
    core, yh, yl = at_ref[0], at_ref[1], at_ref[2]
    for rel in range(2):
        for xh in range(4):
            z = 2 * xh + (core if rel == 0 else 1 - core)
            for q in range(4):
                row = rel * 64 + xh * 16 + q * 4
                left[row : row + 4, :] = far_ref[z, q]
    whole = left[...]
    high = whole.astype(jnp.bfloat16)
    left2[0:128, :] = high
    left2[128:256, :] = (whole - high.astype(jnp.float32)).astype(jnp.bfloat16)
    for y in range(2):
        shard = jnp.where(yl == y, yh, 4)
        for z in range(8):
            for xl in range(2):
                row = z * 8 + xl * 4 + y * 2
                mode_j[row : row + 2, :] = far_ref[z, shard, 2 * xl : 2 * xl + 2, :]
    for xl in range(2):
        for y in range(8):
            row = xl * 16 + y * 2
            slope[row : row + 2, :] = near_ref[xl, y, 2:4, :]

    lane = lax.broadcasted_iota(jnp.int32, (8, 128), 1)
    nt = (((1,), (1,)), ((), ()))

    def group(g, carry):
        modes = mode_j[pl.ds(pl.multiple_of(g * 16, 16), 16), :]
        for j in range(16):
            prod = slope[...] * modes[j : j + 1, :]
            high = prod.astype(jnp.bfloat16)
            prod_hi[j * 32 : (j + 1) * 32, :] = high
            prod_lo[j * 32 : (j + 1) * 32, :] = (prod - high.astype(jnp.float32)).astype(jnp.bfloat16)
        one = lax.dot_general(prod_hi[...], left2[...], nt, preferred_element_type=jnp.float32)
        two = lax.dot_general(prod_lo[...], left2[0:128, :], nt, preferred_element_type=jnp.float32)
        both = one[:, 0:128] + (one[:, 128:256] + two)
        for t in range(4):
            tile = both[t * 128 : (t + 1) * 128, :].T
            z, xl = g * 2 + t // 2, t % 2
            for s in range(8):
                ref, xh = (keep_ref, s) if s < 4 else (send_ref, s - 4)
                top, low = tile[s * 16 : s * 16 + 8, :], tile[s * 16 + 8 : s * 16 + 16, :]
                ref[xh, z, xl, 0] = jnp.where(lane < 64, top, pltpu.roll(low, 64, 1))
                ref[xh, z, xl, 1] = jnp.where(lane < 64, pltpu.roll(top, 64, 1), low)
        return carry

    lax.fori_loop(0, 4, group, 0)


def finish_kernel(factor, parts_ref, out_ref):
    lane = lax.broadcasted_iota(jnp.int32, (8, 128), 1)
    for yl in range(2):
        sums = []
        for z in range(8):
            total = parts_ref[0, z, 0, yl]
            for xh in range(4):
                for xl in range(2):
                    if xh or xl:
                        total = total + parts_ref[xh, z, xl, yl]
            sums.append(total * factor)
        for h in range(2):
            for bj in range(2):
                for side in range(2):
                    wide = None
                    for p in range(4):
                        here = sums[side * 4 + p]
                        shift = (p * 32 - (h * 64 + bj * 32)) % 128
                        moved = pltpu.roll(here, shift, 1) if shift else here
                        wide = moved if wide is None else jnp.where(lane < p * 32, wide, moved)
                    for r in range(8):
                        q, xl, b = h * 2 + r // 4, (r // 2) % 2, r % 2
                        i = xl * 16 + (2 * q + yl) * 2 + b
                        out_ref[i, bj : bj + 1, side * 128 : (side + 1) * 128] = wide[r : r + 1, :]


def per_device(modes_field, slopes):
    rows = modes_field.shape[0]
    half = rows // 2
    f32 = jnp.float32
    shape = jax.ShapeDtypeStruct
    factor = 1.0 / math.sqrt(rows * lax.axis_size(SPACE))
    at = jnp.stack([lax.axis_index("core"), lax.axis_index("yh"), lax.axis_index("yl")]).astype(jnp.int32)
    spread = pl.pallas_call(
        spread_kernel, out_shape=shape((2, 8, 4, half), f32), in_specs=[VMEM, VMEM], out_specs=VMEM
    )(modes_field.T, slopes.T)
    near = lax.all_to_all(spread.reshape(16, 4, half), ("xl", "yh", "yl"), 0, 0, tiled=True)
    near = near.reshape(2, 8, 4, half)
    picked = pl.pallas_call(
        pick_kernel, out_shape=shape((8, 5, 4, half), f32), in_specs=[SMEM, VMEM], out_specs=VMEM
    )(at, near)
    far = lax.all_to_all(picked, "z", 0, 0, tiled=True)
    piece = shape((4, 8, 2, 2, 8, 128), f32)
    keep, send = pl.pallas_call(
        tensor_kernel,
        out_shape=(piece, piece),
        in_specs=[SMEM, VMEM, VMEM],
        out_specs=(VMEM, VMEM),
        scratch_shapes=[
            pltpu.VMEM((128, half), f32),
            pltpu.VMEM((256, half), jnp.bfloat16),
            pltpu.VMEM((64, half), f32),
            pltpu.VMEM((32, half), f32),
            pltpu.VMEM((512, half), jnp.bfloat16),
            pltpu.VMEM((512, half), jnp.bfloat16),
        ],
    )(at, near, far)
    pair = keep + lax.ppermute(send, "core", [(0, 1), (1, 0)])
    parts = lax.all_to_all(pair.reshape(128, 8, 128), ("xh", "z", "xl", "yl"), 0, 0, tiled=True)
    return pl.pallas_call(
        functools.partial(finish_kernel, factor), out_shape=shape((32, 2, 256), f32), in_specs=[VMEM], out_specs=VMEM
    )(parts.reshape(4, 8, 2, 2, 8, 128))


def solution(mesh):
    fine = Mesh(mesh.devices.reshape(4, 2, 8, 2, 4, 2), AXES)
    placed = P(SPACE, MODES)
    return jax.shard_map(
        per_device, mesh=fine, in_specs=(placed, placed), out_specs=P(SPACE, MODES, None), check_vma=False
    )
```

time: 1270 us -> 115 us (0.09)
  waiting for transfers between devices: 1210 us -> 13.8 us
  blocking collectives: 0 us -> 74.4 us
  local copies, waits for them, and re-layouts: 19.6 us -> 0.76 us
  Pallas kernels: 0 us -> 13.1 us
  between operations: 13.1 us -> 0.03 us
  matrix products: 12.8 us -> 0 us
    all_gather x2 -> x0, waiting for transfers between devices: 1180 us -> none  [the longest x1 606 us: per_device(): slope_all = lax.all_gather(slopes, 'modes', axis=1, tiled=True)]
    all_to_all x0 -> x2, blocking collectives: none -> 74.4 us  [the longest x1 41.5 us: per_device(): far = lax.all_to_all(picked, 'z', 0, 0, tiled=True)]
    unnamed x4 -> x0, waiting for transfers between devices: 33.5 us -> none
    unnamed x7 -> x2, local copies, waits for them, and re-layouts: 18.9 us -> 0.76 us
    pallas_call x0 -> x4, Pallas kernels: none -> 13.1 us  [the longest x1 7.58 us: per_device(): pl.pallas_call(tensor_kernel, out_shape=(piece, piece), in_specs=[SMEM, V...]
    dot_general x1 -> x0, matrix products: 12.8 us -> none  [project(): lax.dot_general(panel, weighted, (((0,), (0,)), ((), ())), precision=lax....]
  transfers between devices with their start and end apart: 3 -> 2, of which waited for: 3 -> 2; matrix products, arithmetic and copies ran while one was open for 2% -> 1% of each run, Pallas kernels for 0% -> 0%
where the time goes in v1:
time: 115 us; the launch traced here: 114 us
  blocking collectives  74.4 us (65%)
  waiting for transfers between devices  13.8 us (12%)
  Pallas kernels  13.1 us (11%)
  starting transfers between devices  10.5 us (9%)
  other arithmetic  1.8 us (2%)
    all_to_all x1, blocking collectives, per_device(): far = lax.all_to_all(picked, 'z', 0, 0, tiled=True)  41.5 us
    all_to_all x1, blocking collectives, per_device(): lax.all_to_all(pair.reshape(128, 8, 128), ('xh', 'z', 'xl', 'yl'), 0, 0,...  32.9 us
    all_to_all x1, waiting for transfers between devices, per_device(): lax.all_to_all(spread.reshape(16, 4, half), ('xl', 'yh', 'yl'), 0, 0, til...  11.7 us
    all_to_all x1, starting transfers between devices, per_device(): lax.all_to_all(spread.reshape(16, 4, half), ('xl', 'yh', 'yl'), 0, 0, til...  8.59 us
    pallas_call x1, Pallas kernels, per_device(): pl.pallas_call(tensor_kernel, out_shape=(piece, piece), in_specs=[SMEM, V...  7.58 us
  transfers between devices with their start and end apart: 2, of which 2 were waited for; matrix products, arithmetic and copies ran while one was open for 1% of the time, Pallas kernels for 0%

profile of v1, /device:TPU:4, one launch (start us, length us, event | category | flops | bytes accessed | tf_op | source)
XLA Modules:
  0.0 114.4 jit_solution(11917166811252622126)
XLA Ops:
  0.0 1.6 %shard_map.28 = f32[2,8,4,1536]{3,2,1,0:T(4,128)} custom-call(f32[2,3072]{1,0:T(2,128)} %bitcast.14, f32[2,3072]{1,0:T(2,128)} %bitcast.15), custom_call_target="tpu_custom_call" | custom-call | tf_op jit(solution)/shard_map/pallas_call | solution.py:120
  1.6 8.6 %all-to-all-start = ((f32[16,4,1536]{2,1,0:T(4,128)}), f32[16,4,1536]{2,1,0:T(4,128)S(1)}, u32[]{:S(2)}, u32[]{:S(2)}) async-start(f32[16,4,1536]{2,1,0:T(4,128)} %bitcast.13), calls=%async_computation | async-start | bytes 786432 | tf_op jit(solution)/shard_map/all_to_all | solution.py:123
  10.2 0.7 pad_add_fusion.at_ref
  10.9 11.7 %all-to-all-done = f32[16,4,1536]{2,1,0:T(4,128)S(1)} async-done(((f32[16,4,1536]{2,1,0:T(4,128)}), f32[16,4,1536]{2,1,0:T(4,128)S(1)}, u32[]{:S(2)}, u32[]{:S(2)}) %all-to-all-start) | async-done | bytes 393248 | tf_op jit(solution)/shard_map/all_to_all | solution.py:123
  22.6 0.0 copy-start
  22.6 0.8 copy-done
  23.4 2.1 %shard_map.29 = f32[8,5,4,1536]{3,2,1,0:T(4,128)} custom-call(s32[3]{0:T(128)} %pad_add_fusion.at_ref, f32[2,8,4,1536]{3,2,1,0:T(4,128)} %bitcast.9), custom_call_target="tpu_custom_call" | custom-call | tf_op jit(solution)/shard_map/pallas_call | solution.py:125
  25.5 41.5 %all_to_all.15.far_ref = f32[8,5,4,1536]{3,2,1,0:T(4,128)} all-to-all(f32[8,5,4,1536]{3,2,1,0:T(4,128)} %shard_map.29), channel_id=1, replica_groups=mesh['xh'=4,'core'=2,'z'=8,'xl'=2,'yh'=4,'yl'=2] {'z'}, dimensions={0} | all-to-all | bytes 1966080 | tf_op jit(solution)/shard_map/all_to_all | solution.py:128
  67.0 7.6 %shard_map.30 = (f32[4,8,2,2,8,128]{5,4,3,2,1,0:T(8,128)}, f32[4,8,2,2,8,128]{5,4,3,2,1,0:T(8,128)}) custom-call(s32[3]{0:T(128)} %pad_add_fusion.at_ref, f32[2,8,4,1536]{3,2,1,0:T(4,128)} %bitcast.10, f32[8,5,4,1536]{3,2,1,0:T(4,128)} %all_to_all.15.far_ref), custom_call_target="tpu_custom_call" | custom-call | tf_op jit(solution)/shard_map/pallas_call | solution.py:130
  74.6 1.9 %collective-permute-start = (f32[4,8,2,2,8,128]{5,4,3,2,1,0:T(8,128)}, f32[4,8,2,2,8,128]{5,4,3,2,1,0:T(8,128)S(1)}, u32[]{:S(2)}, u32[]{:S(2)}) collective-permute-start(f32[4,8,2,2,8,128]{5,4,3,2,1,0:T(8,128)} %get-tuple-element.8), channel_id=1, source_target_pairs={{0,128},{128,0},{1,129},{129,1},{2,130},{130,2},{3,131},{131,3},{4... | collective-permute-start | bytes 1572872 | tf_op jit(solution)/shard_map/ppermute | solution.py:144
  76.5 2.1 %collective-permute-done = f32[4,8,2,2,8,128]{5,4,3,2,1,0:T(8,128)S(1)} collective-permute-done((f32[4,8,2,2,8,128]{5,4,3,2,1,0:T(8,128)}, f32[4,8,2,2,8,128]{5,4,3,2,1,0:T(8,128)S(1)}, u32[]{:S(2)}, u32[]{:S(2)}) %collective-permute-start) | collective-permute-done | bytes 524320 | tf_op jit(solution)/shard_map/ppermute | solution.py:144
  78.6 1.1 add.3
  79.7 32.9 %all_to_all.16 = f32[128,8,128]{2,1,0:T(8,128)} all-to-all(f32[128,8,128]{2,1,0:T(8,128)S(1)} %bitcast.11), channel_id=1, replica_groups=mesh['xh'=4,'core'=2,'z'=8,'xl'=2,'yh'=4,'yl'=2] {'xh','z','xl','yl'}, dimensions={0} | all-to-all | bytes 1048576 | tf_op jit(solution)/shard_map/all_to_all | solution.py:145
  112.6 1.8 %shard_map.31 = f32[32,2,256]{2,1,0:T(2,128)} custom-call(f32[4,8,2,2,8,128]{5,4,3,2,1,0:T(8,128)} %bitcast.12), custom_call_target="tpu_custom_call" | custom-call | tf_op jit(solution)/shard_map/pallas_call | solution.py:146
Async XLA Ops:
  1.6 21.0 %all-to-all-start = ((f32[16,4,1536]{2,1,0:T(4,128)}), f32[16,4,1536]{2,1,0:T(4,128)S(1)}, u32[]{:S(2)}, u32[]{:S(2)}) async-start(f32[16,4,1536]{2,1,0:T(4,128)} %bitcast.13), calls=%async_computation | async-start | bytes 786432 | tf_op jit(solution)/shard_map/all_to_all | solution.py:123
  22.6 0.8 copy-start
  74.6 4.0 %collective-permute-start = (f32[4,8,2,2,8,128]{5,4,3,2,1,0:T(8,128)}, f32[4,8,2,2,8,128]{5,4,3,2,1,0:T(8,128)S(1)}, u32[]{:S(2)}, u32[]{:S(2)}) collective-permute-start(f32[4,8,2,2,8,128]{5,4,3,2,1,0:T(8,128)} %get-tuple-element.8), channel_id=1, source_target_pairs={{0,128},{128,0},{1,129},{129,1},{2,130},{130,2},{3,131},{131,3},{4... | collective-permute-start | bytes 1572872 | tf_op jit(solution)/shard_map/ppermute | solution.py:144

commit v2 on v1

--- a/solution.py
+++ b/solution.py
@@ -13,11 +13,28 @@
 SPACE = ("xh", "core")
 MODES = ("z", "xl", "yh", "yl")
 VMEM = pl.BlockSpec(memory_space=pltpu.VMEM)
-SMEM = pl.BlockSpec(memory_space=pltpu.SMEM)
+HBM = pl.BlockSpec(memory_space=pltpu.HBM)
 
 
-def spread_kernel(m_ref, s_ref, out_ref):
+def on_chip(x):
+    return pltpu.with_memory_space_constraint(x, pltpu.VMEM)
+
+
+def in_place(x):
+    return pltpu.with_memory_space_constraint(x, pltpu.HBM)
+
+
+def room(mib):
+    return pltpu.CompilerParams(vmem_limit_bytes=mib << 20)
+
+
+def spread_kernel(m_hbm, s_hbm, out_ref, m_ref, s_ref, sem):
     rows = out_ref.shape[3]
+    copies = [pltpu.make_async_copy(m_hbm, m_ref, sem.at[0]), pltpu.make_async_copy(s_hbm, s_ref, sem.at[1])]
+    for copy in copies:
+        copy.start()
+    for copy in copies:
+        copy.wait()
     for half in range(2):
         cut = slice(half * rows, (half + 1) * rows)
         for y in range(8):
@@ -25,18 +42,17 @@
             out_ref[half, y, 2:4, :] = s_ref[:, cut]
 
 
-def pick_kernel(at_ref, near_ref, out_ref):
-    yh, yl = at_ref[1], at_ref[2]
+def pick_kernel(near_ref, out_ref):
+    yh, yl = lax.axis_index("yh"), lax.axis_index("yl")
     for shard in range(5):
         y = 2 * shard + yl if shard < 4 else 2 * yh + 1 - yl
         for xl in range(2):
             piece = near_ref[xl, y, 0:2, :]
-            for z in range(8):
-                out_ref[z, shard, 2 * xl : 2 * xl + 2, :] = piece
+            out_ref[shard, 2 * xl : 2 * xl + 2, :] = piece
 
 
-def tensor_kernel(at_ref, near_ref, far_ref, keep_ref, send_ref, left, left2, mode_j, slope, prod_hi, prod_lo):
-    core, yh, yl = at_ref[0], at_ref[1], at_ref[2]
+def tensor_kernel(near_ref, far_ref, keep_ref, send_ref, left, left2, mode_j, slope, prod_hi, prod_lo):
+    core, yh, yl = lax.axis_index("core"), lax.axis_index("yh"), lax.axis_index("yl")
     for rel in range(2):
         for xh in range(4):
             z = 2 * xh + (core if rel == 0 else 1 - core)
@@ -111,26 +127,37 @@
 
 
 def per_device(modes_field, slopes):
-    rows = modes_field.shape[0]
+    rows, own = modes_field.shape
     half = rows // 2
     f32 = jnp.float32
-    shape = jax.ShapeDtypeStruct
     factor = 1.0 / math.sqrt(rows * lax.axis_size(SPACE))
-    at = jnp.stack([lax.axis_index("core"), lax.axis_index("yh"), lax.axis_index("yl")]).astype(jnp.int32)
     spread = pl.pallas_call(
-        spread_kernel, out_shape=shape((2, 8, 4, half), f32), in_specs=[VMEM, VMEM], out_specs=VMEM
-    )(modes_field.T, slopes.T)
+        spread_kernel,
+        out_shape=pltpu.VMEM((2, 8, 4, half), f32),
+        in_specs=[HBM, HBM],
+        out_specs=VMEM,
+        scratch_shapes=[
+            pltpu.VMEM((own, rows), f32),
+            pltpu.VMEM((own, rows), f32),
+            pltpu.SemaphoreType.DMA((2,)),
+        ],
+        compiler_params=room(8),
+    )(in_place(modes_field.T), in_place(slopes.T))
     near = lax.all_to_all(spread.reshape(16, 4, half), ("xl", "yh", "yl"), 0, 0, tiled=True)
-    near = near.reshape(2, 8, 4, half)
+    near = on_chip(near.reshape(2, 8, 4, half))
     picked = pl.pallas_call(
-        pick_kernel, out_shape=shape((8, 5, 4, half), f32), in_specs=[SMEM, VMEM], out_specs=VMEM
-    )(at, near)
-    far = lax.all_to_all(picked, "z", 0, 0, tiled=True)
-    piece = shape((4, 8, 2, 2, 8, 128), f32)
+        pick_kernel,
+        out_shape=pltpu.VMEM((5, 4, half), f32),
+        in_specs=[VMEM],
+        out_specs=VMEM,
+        compiler_params=room(8),
+    )(near)
+    far = on_chip(lax.all_gather(picked, "z", axis=0))
+    piece = pltpu.VMEM((4, 8, 2, 2, 8, 128), f32)
     keep, send = pl.pallas_call(
         tensor_kernel,
         out_shape=(piece, piece),
-        in_specs=[SMEM, VMEM, VMEM],
+        in_specs=[VMEM, VMEM],
         out_specs=(VMEM, VMEM),
         scratch_shapes=[
             pltpu.VMEM((128, half), f32),
@@ -140,12 +167,17 @@
             pltpu.VMEM((512, half), jnp.bfloat16),
             pltpu.VMEM((512, half), jnp.bfloat16),
         ],
-    )(at, near, far)
+        compiler_params=room(24),
+    )(near, far)
     pair = keep + lax.ppermute(send, "core", [(0, 1), (1, 0)])
     parts = lax.all_to_all(pair.reshape(128, 8, 128), ("xh", "z", "xl", "yl"), 0, 0, tiled=True)
     return pl.pallas_call(
-        functools.partial(finish_kernel, factor), out_shape=shape((32, 2, 256), f32), in_specs=[VMEM], out_specs=VMEM
-    )(parts.reshape(4, 8, 2, 2, 8, 128))
+        functools.partial(finish_kernel, factor),
+        out_shape=jax.ShapeDtypeStruct((32, 2, 256), f32),
+        in_specs=[VMEM],
+        out_specs=VMEM,
+        compiler_params=room(8),
+    )(on_chip(parts.reshape(4, 8, 2, 2, 8, 128)))
 
 
 def solution(mesh):

time: 115 us -> 103 us (0.90)
  blocking collectives: 74.4 us -> 92.4 us
  waiting for transfers between devices: 13.8 us -> 1.88 us
  starting transfers between devices: 10.5 us -> 1.92 us
  Pallas kernels: 13.1 us -> 6.89 us
  other arithmetic: 1.8 us -> 0.08 us
    all_gather x0 -> x1, blocking collectives: none -> 39.4 us  [per_device(): far = on_chip(lax.all_gather(picked, 'z', axis=0))]
    all_to_all x1, blocking collectives: 41.5 us -> 20.8 us  [per_device(): lax.all_to_all(spread.reshape(16, 4, half), ('xl', 'yh', 'yl'), 0, 0, til...]
    all_to_all x1 -> x0, waiting for transfers between devices: 11.7 us -> none  [per_device(): lax.all_to_all(spread.reshape(16, 4, half), ('xl', 'yh', 'yl'), 0, 0, til...]
    all_to_all x1 -> x0, starting transfers between devices: 8.59 us -> none  [per_device(): lax.all_to_all(spread.reshape(16, 4, half), ('xl', 'yh', 'yl'), 0, 0, til...]
    pallas_call x4, Pallas kernels: 13.1 us -> 6.89 us  [the longest x1 5.21 us: per_device(): pl.pallas_call(tensor_kernel, out_shape=(piece, piece), in_specs=[VMEM, V...]
  transfers between devices with their start and end apart: 2 -> 1, of which waited for: 2 -> 1; matrix products, arithmetic and copies ran while one was open for 1% -> 0% of each run, Pallas kernels for 0% -> 0%
where the time goes in v2:
time: 103 us
  blocking collectives  92.4 us (90%)
  Pallas kernels  6.89 us (7%)
  starting transfers between devices  1.92 us (2%)
  waiting for transfers between devices  1.88 us (2%)
    all_gather x1, blocking collectives, per_device(): far = on_chip(lax.all_gather(picked, 'z', axis=0))  39.4 us
    all_to_all x1, blocking collectives, per_device(): lax.all_to_all(pair.reshape(128, 8, 128), ('xh', 'z', 'xl', 'yl'), 0, 0,...  32.2 us
    all_to_all x1, blocking collectives, per_device(): lax.all_to_all(spread.reshape(16, 4, half), ('xl', 'yh', 'yl'), 0, 0, til...  20.8 us
    pallas_call x1, Pallas kernels, per_device(): pl.pallas_call(tensor_kernel, out_shape=(piece, piece), in_specs=[VMEM, V...  5.21 us
  transfers between devices with their start and end apart: 1, of which 1 were waited for; matrix products, arithmetic and copies ran while one was open for 0% of the time, Pallas kernels for 0%

profile of v2, /device:TPU:4, one launch (start us, length us, event | category | flops | bytes accessed | tf_op | source)
XLA Modules:
  0.0 103.2 jit_solution(11050660750910963965)
XLA Ops:
  0.0 0.9 shard_map.28
  0.9 20.8 %all_to_all.10 = f32[16,4,1536]{2,1,0:T(4,128)S(1)} all-to-all(f32[16,4,1536]{2,1,0:T(4,128)S(1)} %bitcast.11), channel_id=1, replica_groups=mesh['xh'=4,'core'=2,'z'=8,'xl'=2,'yh'=4,'yl'=2] {'xl','yh','yl'}, dimensions={0} | all-to-all | bytes 786432 | tf_op jit(solution)/shard_map/all_to_all | solution.py:146
  21.7 39.4 %all-gather = f32[40,4,1536]{2,1,0:T(4,128)S(1)} all-gather(f32[5,4,1536]{2,1,0:T(4,128)S(1)} %shard_map.29), channel_id=2, replica_groups=mesh['xh'=4,'core'=2,'z'=8,'xl'=2,'yh'=4,'yl'=2] {'z'}, dimensions={0}, use_global_device_ids=true | all-gather | bytes 1105920 | tf_op jit(solution)/shard_map/all_gather | solution.py:155
  61.1 5.2 %shard_map.30 = (f32[4,8,2,2,8,128]{5,4,3,2,1,0:T(8,128)S(1)}, f32[4,8,2,2,8,128]{5,4,3,2,1,0:T(8,128)S(1)}) custom-call(f32[2,8,4,1536]{3,2,1,0:T(4,128)S(1)} %bitcast.9, f32[8,5,4,1536]{3,2,1,0:T(4,128)S(1)} %bitcast.7), custom_call_target="tpu_custom_call" | custom-call | tf_op jit(solution)/shard_map/pallas_call | solution.py:157
  66.3 1.9 %collective-permute-start = (f32[4,8,2,2,8,128]{5,4,3,2,1,0:T(8,128)S(1)}, f32[4,8,2,2,8,128]{5,4,3,2,1,0:T(8,128)S(1)}, u32[]{:S(2)}, u32[]{:S(2)}) collective-permute-start(f32[4,8,2,2,8,128]{5,4,3,2,1,0:T(8,128)S(1)} %get-tuple-element.8), channel_id=1, source_target_pairs={{0,128},{128,0},{1,129},{129,1},{2,130},{130,2},{3,131},{131,3},{4... | collective-permute-start | bytes 1572872 | tf_op jit(solution)/shard_map/ppermute | solution.py:172
  68.3 1.9 %collective-permute-done = f32[4,8,2,2,8,128]{5,4,3,2,1,0:T(8,128)S(1)} collective-permute-done((f32[4,8,2,2,8,128]{5,4,3,2,1,0:T(8,128)S(1)}, f32[4,8,2,2,8,128]{5,4,3,2,1,0:T(8,128)S(1)}, u32[]{:S(2)}, u32[]{:S(2)}) %collective-permute-start) | collective-permute-done | bytes 524320 | tf_op jit(solution)/shard_map/ppermute | solution.py:172
  70.1 0.1 add.3
  70.2 32.2 %all_to_all.11 = f32[128,8,128]{2,1,0:T(8,128)S(1)} all-to-all(f32[128,8,128]{2,1,0:T(8,128)S(1)} %bitcast.12), channel_id=1, replica_groups=mesh['xh'=4,'core'=2,'z'=8,'xl'=2,'yh'=4,'yl'=2] {'xh','z','xl','yl'}, dimensions={0} | all-to-all | bytes 1048576 | tf_op jit(solution)/shard_map/all_to_all | solution.py:173
  102.4 0.8 shard_map.31
  (1 shorter events, 0.0 us)
Async XLA Ops:
  66.3 3.8 %collective-permute-start = (f32[4,8,2,2,8,128]{5,4,3,2,1,0:T(8,128)S(1)}, f32[4,8,2,2,8,128]{5,4,3,2,1,0:T(8,128)S(1)}, u32[]{:S(2)}, u32[]{:S(2)}) collective-permute-start(f32[4,8,2,2,8,128]{5,4,3,2,1,0:T(8,128)S(1)} %get-tuple-element.8), channel_id=1, source_target_pairs={{0,128},{128,0},{1,129},{129,1},{2,130},{130,2},{3,131},{131,3},{4... | collective-permute-start | bytes 1572872 | tf_op jit(solution)/shard_map/ppermute | solution.py:172

commit v3 on v2

--- a/solution.py
+++ b/solution.py
@@ -77,27 +77,25 @@
     lane = lax.broadcasted_iota(jnp.int32, (8, 128), 1)
     nt = (((1,), (1,)), ((), ()))
 
-    def group(g, carry):
-        modes = mode_j[pl.ds(pl.multiple_of(g * 16, 16), 16), :]
-        for j in range(16):
+    for g in range(2):
+        high_ref, low_ref = prod_hi.at[g % 2], prod_lo.at[g % 2]
+        modes = mode_j[g * 32 : (g + 1) * 32, :]
+        for j in range(32):
             prod = slope[...] * modes[j : j + 1, :]
             high = prod.astype(jnp.bfloat16)
-            prod_hi[j * 32 : (j + 1) * 32, :] = high
-            prod_lo[j * 32 : (j + 1) * 32, :] = (prod - high.astype(jnp.float32)).astype(jnp.bfloat16)
-        one = lax.dot_general(prod_hi[...], left2[...], nt, preferred_element_type=jnp.float32)
-        two = lax.dot_general(prod_lo[...], left2[0:128, :], nt, preferred_element_type=jnp.float32)
+            high_ref[j * 32 : (j + 1) * 32, :] = high
+            low_ref[j * 32 : (j + 1) * 32, :] = (prod - high.astype(jnp.float32)).astype(jnp.bfloat16)
+        one = lax.dot_general(high_ref[...], left2[...], nt, preferred_element_type=jnp.float32)
+        two = lax.dot_general(low_ref[...], left2[0:128, :], nt, preferred_element_type=jnp.float32)
         both = one[:, 0:128] + (one[:, 128:256] + two)
-        for t in range(4):
+        for t in range(8):
             tile = both[t * 128 : (t + 1) * 128, :].T
-            z, xl = g * 2 + t // 2, t % 2
+            z, xl = g * 4 + t // 2, t % 2
             for s in range(8):
                 ref, xh = (keep_ref, s) if s < 4 else (send_ref, s - 4)
                 top, low = tile[s * 16 : s * 16 + 8, :], tile[s * 16 + 8 : s * 16 + 16, :]
                 ref[xh, z, xl, 0] = jnp.where(lane < 64, top, pltpu.roll(low, 64, 1))
                 ref[xh, z, xl, 1] = jnp.where(lane < 64, pltpu.roll(top, 64, 1), low)
-        return carry
-
-    lax.fori_loop(0, 4, group, 0)
 
 
 def finish_kernel(factor, parts_ref, out_ref):
@@ -164,8 +162,8 @@
             pltpu.VMEM((256, half), jnp.bfloat16),
             pltpu.VMEM((64, half), f32),
             pltpu.VMEM((32, half), f32),
-            pltpu.VMEM((512, half), jnp.bfloat16),
-            pltpu.VMEM((512, half), jnp.bfloat16),
+            pltpu.VMEM((2, 1024, half), jnp.bfloat16),
+            pltpu.VMEM((2, 1024, half), jnp.bfloat16),
         ],
         compiler_params=room(24),
     )(near, far)

time: 103 us -> 102 us (level)
  Pallas kernels: 6.89 us -> 5.37 us
    pallas_call x1, Pallas kernels: 5.21 us -> 3.7 us  [per_device(): pl.pallas_call(tensor_kernel, out_shape=(piece, piece), in_specs=[VMEM, V...]
where the time goes in v3:
time: 102 us
  blocking collectives  92.4 us (91%)
  Pallas kernels  5.37 us (5%)
  starting transfers between devices  1.92 us (2%)
  waiting for transfers between devices  1.88 us (2%)
    all_gather x1, blocking collectives, per_device(): far = on_chip(lax.all_gather(picked, 'z', axis=0))  39.4 us
    all_to_all x1, blocking collectives, per_device(): lax.all_to_all(pair.reshape(128, 8, 128), ('xh', 'z', 'xl', 'yl'), 0, 0,...  32.2 us
    all_to_all x1, blocking collectives, per_device(): lax.all_to_all(spread.reshape(16, 4, half), ('xl', 'yh', 'yl'), 0, 0, til...  20.8 us
    pallas_call x1, Pallas kernels, per_device(): pl.pallas_call(tensor_kernel, out_shape=(piece, piece), in_specs=[VMEM, V...  3.7 us
  transfers between devices with their start and end apart: 1, of which 1 were waited for; matrix products, arithmetic and copies ran while one was open for 0% of the time, Pallas kernels for 0%

profile of v3, /device:TPU:4, one launch (start us, length us, event | category | flops | bytes accessed | tf_op | source)
XLA Modules:
  0.0 101.7 jit_solution(9926380115595330069)
XLA Ops:
  0.0 0.9 shard_map.28
  0.9 20.8 %all_to_all.10 = f32[16,4,1536]{2,1,0:T(4,128)S(1)} all-to-all(f32[16,4,1536]{2,1,0:T(4,128)S(1)} %bitcast.11), channel_id=1, replica_groups=mesh['xh'=4,'core'=2,'z'=8,'xl'=2,'yh'=4,'yl'=2] {'xl','yh','yl'}, dimensions={0} | all-to-all | bytes 786432 | tf_op jit(solution)/shard_map/all_to_all | solution.py:144
  21.7 39.4 %all-gather = f32[40,4,1536]{2,1,0:T(4,128)S(1)} all-gather(f32[5,4,1536]{2,1,0:T(4,128)S(1)} %shard_map.29), channel_id=2, replica_groups=mesh['xh'=4,'core'=2,'z'=8,'xl'=2,'yh'=4,'yl'=2] {'z'}, dimensions={0}, use_global_device_ids=true | all-gather | bytes 1105920 | tf_op jit(solution)/shard_map/all_gather | solution.py:153
  61.1 3.7 %shard_map.30 = (f32[4,8,2,2,8,128]{5,4,3,2,1,0:T(8,128)S(1)}, f32[4,8,2,2,8,128]{5,4,3,2,1,0:T(8,128)S(1)}) custom-call(f32[2,8,4,1536]{3,2,1,0:T(4,128)S(1)} %bitcast.9, f32[8,5,4,1536]{3,2,1,0:T(4,128)S(1)} %bitcast.7), custom_call_target="tpu_custom_call" | custom-call | tf_op jit(solution)/shard_map/pallas_call | solution.py:155
  64.8 1.9 %collective-permute-start = (f32[4,8,2,2,8,128]{5,4,3,2,1,0:T(8,128)S(1)}, f32[4,8,2,2,8,128]{5,4,3,2,1,0:T(8,128)S(1)}, u32[]{:S(2)}, u32[]{:S(2)}) collective-permute-start(f32[4,8,2,2,8,128]{5,4,3,2,1,0:T(8,128)S(1)} %get-tuple-element.8), channel_id=1, source_target_pairs={{0,128},{128,0},{1,129},{129,1},{2,130},{130,2},{3,131},{131,3},{4... | collective-permute-start | bytes 1572872 | tf_op jit(solution)/shard_map/ppermute | solution.py:170
  66.7 1.9 %collective-permute-done = f32[4,8,2,2,8,128]{5,4,3,2,1,0:T(8,128)S(1)} collective-permute-done((f32[4,8,2,2,8,128]{5,4,3,2,1,0:T(8,128)S(1)}, f32[4,8,2,2,8,128]{5,4,3,2,1,0:T(8,128)S(1)}, u32[]{:S(2)}, u32[]{:S(2)}) %collective-permute-start) | collective-permute-done | bytes 524320 | tf_op jit(solution)/shard_map/ppermute | solution.py:170
  68.6 0.1 add.3
  68.7 32.2 %all_to_all.11 = f32[128,8,128]{2,1,0:T(8,128)S(1)} all-to-all(f32[128,8,128]{2,1,0:T(8,128)S(1)} %bitcast.12), channel_id=1, replica_groups=mesh['xh'=4,'core'=2,'z'=8,'xl'=2,'yh'=4,'yl'=2] {'xh','z','xl','yl'}, dimensions={0} | all-to-all | bytes 1048576 | tf_op jit(solution)/shard_map/all_to_all | solution.py:171
  100.9 0.8 shard_map.31
  (1 shorter events, 0.0 us)
Async XLA Ops:
  64.8 3.8 %collective-permute-start = (f32[4,8,2,2,8,128]{5,4,3,2,1,0:T(8,128)S(1)}, f32[4,8,2,2,8,128]{5,4,3,2,1,0:T(8,128)S(1)}, u32[]{:S(2)}, u32[]{:S(2)}) collective-permute-start(f32[4,8,2,2,8,128]{5,4,3,2,1,0:T(8,128)S(1)} %get-tuple-element.8), channel_id=1, source_target_pairs={{0,128},{128,0},{1,129},{129,1},{2,130},{130,2},{3,131},{131,3},{4... | collective-permute-start | bytes 1572872 | tf_op jit(solution)/shard_map/ppermute | solution.py:170

commit v4 on v3

--- a/solution.py
+++ b/solution.py
@@ -53,6 +53,7 @@
 
 def tensor_kernel(near_ref, far_ref, keep_ref, send_ref, left, left2, mode_j, slope, prod_hi, prod_lo):
     core, yh, yl = lax.axis_index("core"), lax.axis_index("yh"), lax.axis_index("yl")
+    own_xl = lax.axis_index("xl")
     for rel in range(2):
         for xh in range(4):
             z = 2 * xh + (core if rel == 0 else 1 - core)
@@ -90,12 +91,18 @@
         both = one[:, 0:128] + (one[:, 128:256] + two)
         for t in range(8):
             tile = both[t * 128 : (t + 1) * 128, :].T
-            z, xl = g * 4 + t // 2, t % 2
+            z, side = g * 4 + t // 2, jnp.where(own_xl == t % 2, 0, 1)
             for s in range(8):
                 ref, xh = (keep_ref, s) if s < 4 else (send_ref, s - 4)
                 top, low = tile[s * 16 : s * 16 + 8, :], tile[s * 16 + 8 : s * 16 + 16, :]
-                ref[xh, z, xl, 0] = jnp.where(lane < 64, top, pltpu.roll(low, 64, 1))
-                ref[xh, z, xl, 1] = jnp.where(lane < 64, pltpu.roll(top, 64, 1), low)
+                ref[side, xh, z, 0] = jnp.where(lane < 64, top, pltpu.roll(low, 64, 1))
+                ref[side, xh, z, 1] = jnp.where(lane < 64, pltpu.roll(top, 64, 1), low)
+
+
+def join_kernel(keep_ref, here_ref, left_ref, right_ref, out_ref):
+    for half, ref in ((0, left_ref), (1, right_ref)):
+        cut = slice(2 * half, 2 * half + 2)
+        out_ref[cut] = keep_ref[0, cut] + here_ref[0, cut] + ref[...]
 
 
 def finish_kernel(factor, parts_ref, out_ref):
@@ -103,11 +110,9 @@
     for yl in range(2):
         sums = []
         for z in range(8):
-            total = parts_ref[0, z, 0, yl]
-            for xh in range(4):
-                for xl in range(2):
-                    if xh or xl:
-                        total = total + parts_ref[xh, z, xl, yl]
+            total = parts_ref[0, z, yl]
+            for xh in range(1, 4):
+                total = total + parts_ref[xh, z, yl]
             sums.append(total * factor)
         for h in range(2):
             for bj in range(2):
@@ -151,7 +156,7 @@
         compiler_params=room(8),
     )(near)
     far = on_chip(lax.all_gather(picked, "z", axis=0))
-    piece = pltpu.VMEM((4, 8, 2, 2, 8, 128), f32)
+    piece = pltpu.VMEM((2, 4, 8, 2, 8, 128), f32)
     keep, send = pl.pallas_call(
         tensor_kernel,
         out_shape=(piece, piece),
@@ -167,15 +172,25 @@
         ],
         compiler_params=room(24),
     )(near, far)
-    pair = keep + lax.ppermute(send, "core", [(0, 1), (1, 0)])
-    parts = lax.all_to_all(pair.reshape(128, 8, 128), ("xh", "z", "xl", "yl"), 0, 0, tiled=True)
+    here = lax.ppermute(send, "core", [(0, 1), (1, 0)])
+    chips = 2 * lax.axis_size("xh")
+    left = lax.ppermute(keep[1, :2] + here[1, :2], ("xh", "xl"), [(x, (x + 1) % chips) for x in range(chips)])
+    right = lax.ppermute(keep[1, 2:] + here[1, 2:], ("xh", "xl"), [((x + 1) % chips, x) for x in range(chips)])
+    pair = pl.pallas_call(
+        join_kernel,
+        out_shape=pltpu.VMEM((4, 8, 2, 8, 128), f32),
+        in_specs=[VMEM] * 4,
+        out_specs=VMEM,
+        compiler_params=room(8),
+    )(*map(on_chip, (keep, here, left, right)))
+    parts = lax.all_to_all(pair.reshape(64, 8, 128), ("xh", "z", "yl"), 0, 0, tiled=True)
     return pl.pallas_call(
         functools.partial(finish_kernel, factor),
         out_shape=jax.ShapeDtypeStruct((32, 2, 256), f32),
         in_specs=[VMEM],
         out_specs=VMEM,
         compiler_params=room(8),
-    )(on_chip(parts.reshape(4, 8, 2, 2, 8, 128)))
+    )(on_chip(parts.reshape(4, 8, 2, 8, 128)))
 
 
 def solution(mesh):

time: 102 us -> 105 us (1.029)
  the two profiles are of different devices: /device:TPU:4 before, /device:TPU:16 now
where the time goes in v4:
time: 105 us
  blocking collectives  83 us (79%)
  waiting for transfers between devices  8.31 us (8%)
  starting transfers between devices  8.09 us (8%)
  Pallas kernels  5.41 us (5%)
    all_gather x1, blocking collectives, per_device(): far = on_chip(lax.all_gather(picked, 'z', axis=0))  36.3 us
    all_to_all x1, blocking collectives, per_device(): lax.all_to_all(spread.reshape(16, 4, half), ('xl', 'yh', 'yl'), 0, 0, til...  25.1 us
    all_to_all x1, blocking collectives, per_device(): lax.all_to_all(pair.reshape(64, 8, 128), ('xh', 'z', 'yl'), 0, 0, tiled=T...  21.5 us
    ppermute x1, waiting for transfers between devices, per_device(): lax.ppermute(keep[1, :2] + here[1, :2], ('xh', 'xl'), [(x, (x + 1) % chip...  5.19 us
    ppermute x1, starting transfers between devices, per_device(): lax.ppermute(keep[1, 2:] + here[1, 2:], ('xh', 'xl'), [((x + 1) % chips,...  4.25 us
    pallas_call x1, Pallas kernels, per_device(): pl.pallas_call(tensor_kernel, out_shape=(piece, piece), in_specs=[VMEM, V...  3.7 us
  transfers between devices with their start and end apart: 3, of which 3 were waited for; matrix products, arithmetic and copies ran while one was open for 0% of the time, Pallas kernels for 0%

profile of v4, /device:TPU:16, one launch (start us, length us, event | category | flops | bytes accessed | tf_op | source)
XLA Modules:
  0.0 104.9 jit_solution(3107694097158465997)
XLA Ops:
  0.0 0.9 shard_map.28
  0.9 25.1 %all_to_all.10 = f32[16,4,1536]{2,1,0:T(4,128)S(1)} all-to-all(f32[16,4,1536]{2,1,0:T(4,128)S(1)} %bitcast.14), channel_id=1, replica_groups=mesh['xh'=4,'core'=2,'z'=8,'xl'=2,'yh'=4,'yl'=2] {'xl','yh','yl'}, dimensions={0} | all-to-all | bytes 786432 | tf_op jit(solution)/shard_map/all_to_all | solution.py:149
  26.0 36.3 %all-gather = f32[40,4,1536]{2,1,0:T(4,128)S(1)} all-gather(f32[5,4,1536]{2,1,0:T(4,128)S(1)} %shard_map.29), channel_id=2, replica_groups=mesh['xh'=4,'core'=2,'z'=8,'xl'=2,'yh'=4,'yl'=2] {'z'}, dimensions={0}, use_global_device_ids=true | all-gather | bytes 1105920 | tf_op jit(solution)/shard_map/all_gather | solution.py:158
  62.3 3.7 %shard_map.30 = (f32[2,4,8,2,8,128]{5,4,3,2,1,0:T(8,128)S(1)}, f32[2,4,8,2,8,128]{5,4,3,2,1,0:T(8,128)S(1)}) custom-call(f32[2,8,4,1536]{3,2,1,0:T(4,128)S(1)} %bitcast.13, f32[8,5,4,1536]{3,2,1,0:T(4,128)S(1)} %bitcast.11), custom_call_target="tpu_custom_call" | custom-call | tf_op jit(solution)/shard_map/pallas_call | solution.py:160
  66.0 1.9 %collective-permute-start = (f32[2,4,8,2,8,128]{5,4,3,2,1,0:T(8,128)S(1)}, f32[2,4,8,2,8,128]{5,4,3,2,1,0:T(8,128)S(1)}, u32[]{:S(2)}, u32[]{:S(2)}) collective-permute-start(f32[2,4,8,2,8,128]{5,4,3,2,1,0:T(8,128)S(1)} %get-tuple-element.8), channel_id=1, source_target_pairs={{0,128},{128,0},{1,129},{129,1},{2,130},{130,2},{3,131},{131,3},{4... | collective-permute-start | bytes 1572872 | tf_op jit(solution)/shard_map/ppermute | solution.py:175
  68.0 1.9 %collective-permute-done.here_ref = f32[2,4,8,2,8,128]{5,4,3,2,1,0:T(8,128)S(1)} collective-permute-done((f32[2,4,8,2,8,128]{5,4,3,2,1,0:T(8,128)S(1)}, f32[2,4,8,2,8,128]{5,4,3,2,1,0:T(8,128)S(1)}, u32[]{:S(2)}, u32[]{:S(2)}) %collective-permute-start) | collective-permute-done | bytes 524320 | tf_op jit(solution)/shard_map/ppermute | solution.py:175
  69.9 4.3 %collective-permute-start.2 = (f32[2,8,2,8,128]{4,3,2,1,0:T(8,128)S(1)}, f32[2,8,2,8,128]{4,3,2,1,0:T(8,128)S(1)}, u32[]{:S(2)}, u32[]{:S(2)}) collective-permute-start(f32[2,8,2,8,128]{4,3,2,1,0:T(8,128)S(1)} %get-tuple-element.9), channel_id=1, source_target_pairs={{8,0},{256,8},{264,256},{512,264},{520,512},{768,520},{776,768},{0... | collective-permute-start | bytes 393224 | tf_op jit(solution)/shard_map/ppermute | solution.py:178
  74.1 1.9 %collective-permute-start.1 = (f32[2,8,2,8,128]{4,3,2,1,0:T(8,128)S(1)}, f32[2,8,2,8,128]{4,3,2,1,0:T(8,128)S(1)}, u32[]{:S(2)}, u32[]{:S(2)}) collective-permute-start(f32[2,8,2,8,128]{4,3,2,1,0:T(8,128)S(1)} %get-tuple-element.10), channel_id=1, source_target_pairs={{0,8},{8,256},{256,264},{264,512},{512,520},{520,768},{768,776},{7... | collective-permute-start | bytes 393224 | tf_op jit(solution)/shard_map/ppermute | solution.py:177
  76.1 1.2 %collective-permute-done.2.right_ref = f32[2,8,2,8,128]{4,3,2,1,0:T(8,128)S(1)} collective-permute-done((f32[2,8,2,8,128]{4,3,2,1,0:T(8,128)S(1)}, f32[2,8,2,8,128]{4,3,2,1,0:T(8,128)S(1)}, u32[]{:S(2)}, u32[]{:S(2)}) %collective-permute-start.2) | collective-permute-done | bytes 131104 | tf_op jit(solution)/shard_map/ppermute | solution.py:178
  77.3 5.2 %collective-permute-done.1.left_ref = f32[2,8,2,8,128]{4,3,2,1,0:T(8,128)S(1)} collective-permute-done((f32[2,8,2,8,128]{4,3,2,1,0:T(8,128)S(1)}, f32[2,8,2,8,128]{4,3,2,1,0:T(8,128)S(1)}, u32[]{:S(2)}, u32[]{:S(2)}) %collective-permute-start.1) | collective-permute-done | bytes 131104 | tf_op jit(solution)/shard_map/ppermute | solution.py:177
  82.6 21.5 %all_to_all.11 = f32[64,8,128]{2,1,0:T(8,128)S(1)} all-to-all(f32[64,8,128]{2,1,0:T(8,128)S(1)} %bitcast.16), channel_id=1, replica_groups=mesh['xh'=4,'core'=2,'z'=8,'xl'=2,'yh'=4,'yl'=2] {'xh','z','yl'}, dimensions={0} | all-to-all | bytes 524288 | tf_op jit(solution)/shard_map/all_to_all | solution.py:186
  104.1 0.8 shard_map.32
  (3 shorter events, 0.1 us)
Async XLA Ops:
  66.0 3.8 %collective-permute-start = (f32[2,4,8,2,8,128]{5,4,3,2,1,0:T(8,128)S(1)}, f32[2,4,8,2,8,128]{5,4,3,2,1,0:T(8,128)S(1)}, u32[]{:S(2)}, u32[]{:S(2)}) collective-permute-start(f32[2,4,8,2,8,128]{5,4,3,2,1,0:T(8,128)S(1)} %get-tuple-element.8), channel_id=1, source_target_pairs={{0,128},{128,0},{1,129},{129,1},{2,130},{130,2},{3,131},{131,3},{4... | collective-permute-start | bytes 1572872 | tf_op jit(solution)/shard_map/ppermute | solution.py:175
  69.9 7.4 %collective-permute-start.2 = (f32[2,8,2,8,128]{4,3,2,1,0:T(8,128)S(1)}, f32[2,8,2,8,128]{4,3,2,1,0:T(8,128)S(1)}, u32[]{:S(2)}, u32[]{:S(2)}) collective-permute-start(f32[2,8,2,8,128]{4,3,2,1,0:T(8,128)S(1)} %get-tuple-element.9), channel_id=1, source_target_pairs={{8,0},{256,8},{264,256},{512,264},{520,512},{768,520},{776,768},{0... | collective-permute-start | bytes 393224 | tf_op jit(solution)/shard_map/ppermute | solution.py:178
  74.1 8.4 %collective-permute-start.1 = (f32[2,8,2,8,128]{4,3,2,1,0:T(8,128)S(1)}, f32[2,8,2,8,128]{4,3,2,1,0:T(8,128)S(1)}, u32[]{:S(2)}, u32[]{:S(2)}) collective-permute-start(f32[2,8,2,8,128]{4,3,2,1,0:T(8,128)S(1)} %get-tuple-element.10), channel_id=1, source_target_pairs={{0,8},{8,256},{256,264},{264,512},{512,520},{520,768},{768,776},{7... | collective-permute-start | bytes 393224 | tf_op jit(solution)/shard_map/ppermute | solution.py:177

commit v5 on v3

--- a/solution.py
+++ b/solution.py
@@ -43,37 +43,59 @@
 
 
 def pick_kernel(near_ref, out_ref):
-    yh, yl = lax.axis_index("yh"), lax.axis_index("yl")
-    for shard in range(5):
-        y = 2 * shard + yl if shard < 4 else 2 * yh + 1 - yl
+    core, yh, yl = lax.axis_index("core"), lax.axis_index("yh"), lax.axis_index("yl")
+    z = lax.axis_index("z")
+
+    def put(piece, p, column):
         for xl in range(2):
-            piece = near_ref[xl, y, 0:2, :]
-            out_ref[shard, 2 * xl : 2 * xl + 2, :] = piece
+            data = near_ref[xl, p, column : column + 2, :]
+            for peer in range(8):
+                out_ref[peer, piece, 2 * xl : 2 * xl + 2, :] = data
+
+    for piece in range(8):
+        y = 2 * piece + yl if piece < 4 else 2 * yh + 1 - yl
+        put(piece, jnp.where(core == 0, y, piece), 0)
+    put(8, z, 2)
 
 
 def tensor_kernel(near_ref, far_ref, keep_ref, send_ref, left, left2, mode_j, slope, prod_hi, prod_lo):
     core, yh, yl = lax.axis_index("core"), lax.axis_index("yh"), lax.axis_index("yl")
+
+    def far(z, y, piece):
+        return jnp.where(core == 0, z, y), jnp.where(core == 0, piece, z)
+
     for rel in range(2):
         for xh in range(4):
             z = 2 * xh + (core if rel == 0 else 1 - core)
             for q in range(4):
                 row = rel * 64 + xh * 16 + q * 4
-                left[row : row + 4, :] = far_ref[z, q]
+                peer, piece = far(z, 2 * q + yl, q)
+                left[row : row + 4, :] = far_ref[peer, piece]
+    for y in range(2):
+        for z in range(8):
+            peer, piece = far(z, 2 * yh + y, jnp.where(yl == y, yh, 4))
+            for xl in range(2):
+                row = z * 8 + xl * 4 + y * 2
+                mode_j[row : row + 2, :] = far_ref[peer, piece, 2 * xl : 2 * xl + 2, :]
+
+    @pl.when(core == 0)
+    def _():
+        for xl in range(2):
+            for y in range(8):
+                row = xl * 16 + y * 2
+                slope[row : row + 2, :] = near_ref[xl, y, 2:4, :]
+
+    @pl.when(core != 0)
+    def _():
+        for xl in range(2):
+            for y in range(8):
+                row = xl * 16 + y * 2
+                slope[row : row + 2, :] = far_ref[y, 8, 2 * xl : 2 * xl + 2, :]
+
     whole = left[...]
     high = whole.astype(jnp.bfloat16)
     left2[0:128, :] = high
     left2[128:256, :] = (whole - high.astype(jnp.float32)).astype(jnp.bfloat16)
-    for y in range(2):
-        shard = jnp.where(yl == y, yh, 4)
-        for z in range(8):
-            for xl in range(2):
-                row = z * 8 + xl * 4 + y * 2
-                mode_j[row : row + 2, :] = far_ref[z, shard, 2 * xl : 2 * xl + 2, :]
-    for xl in range(2):
-        for y in range(8):
-            row = xl * 16 + y * 2
-            slope[row : row + 2, :] = near_ref[xl, y, 2:4, :]
-
     lane = lax.broadcasted_iota(jnp.int32, (8, 128), 1)
     nt = (((1,), (1,)), ((), ()))
 
@@ -124,6 +146,30 @@
                         out_ref[i, bj : bj + 1, side * 128 : (side + 1) * 128] = wide[r : r + 1, :]
 
 
+def gather_groups():
+    first, second = [], []
+    for xh in range(4):
+        for core in range(2):
+            for kept in range(8):
+                for xl in range(2):
+                    line = []
+                    for moved in range(8):
+                        z, y = (kept, moved) if core == 0 else (moved, kept)
+                        line.append((((xh * 2 + core) * 8 + z) * 2 + xl) * 8 + y)
+                    first.append(line)
+    first = [first[n] + first[n + 1] for n in range(0, len(first), 2)]
+    for xh in range(4):
+        for core in range(2):
+            for xl in range(2):
+                for kept in range(8):
+                    line = []
+                    for moved in range(8):
+                        z, y = (moved, kept) if core == 0 else (kept, moved)
+                        line.append((((xh * 2 + core) * 8 + z) * 2 + xl) * 8 + y)
+                    second.append(line)
+    return first, second
+
+
 def per_device(modes_field, slopes):
     rows, own = modes_field.shape
     half = rows // 2
@@ -141,16 +187,17 @@
         ],
         compiler_params=room(8),
     )(in_place(modes_field.T), in_place(slopes.T))
-    near = lax.all_to_all(spread.reshape(16, 4, half), ("xl", "yh", "yl"), 0, 0, tiled=True)
+    first, second = gather_groups()
+    near = lax.all_to_all(spread.reshape(16, 4, half), AXES, 0, 0, axis_index_groups=first, tiled=True)
     near = on_chip(near.reshape(2, 8, 4, half))
     picked = pl.pallas_call(
         pick_kernel,
-        out_shape=pltpu.VMEM((5, 4, half), f32),
+        out_shape=pltpu.VMEM((8, 9, 4, half), f32),
         in_specs=[VMEM],
         out_specs=VMEM,
         compiler_params=room(8),
     )(near)
-    far = on_chip(lax.all_gather(picked, "z", axis=0))
+    far = on_chip(lax.all_to_all(picked, AXES, 0, 0, axis_index_groups=second, tiled=True))
     piece = pltpu.VMEM((4, 8, 2, 2, 8, 128), f32)
     keep, send = pl.pallas_call(
         tensor_kernel,

time: 102 us -> 102 us (level)
    all_to_all x1 -> x2, blocking collectives: 20.8 us -> 61.6 us  [the longest x1 43.7 us: per_device(): lax.all_to_all(picked, AXES, 0, 0, axis_index_groups=second, tiled=True)]
    all_gather x1 -> x0, blocking collectives: 39.4 us -> none  [per_device(): far = on_chip(lax.all_gather(picked, 'z', axis=0))]
    all_to_all x1, blocking collectives: 32.2 us -> 29.9 us  [per_device(): lax.all_to_all(pair.reshape(128, 8, 128), ('xh', 'z', 'xl', 'yl'), 0, 0,...]
where the time goes in v5:
time: 102 us; the launch traced here: 101 us
  blocking collectives  91.5 us (90%)
  Pallas kernels  5.78 us (6%)
  starting transfers between devices  1.92 us (2%)
  waiting for transfers between devices  1.88 us (2%)
    all_to_all x1, blocking collectives, per_device(): lax.all_to_all(picked, AXES, 0, 0, axis_index_groups=second, tiled=True)  43.7 us
    all_to_all x1, blocking collectives, per_device(): lax.all_to_all(pair.reshape(128, 8, 128), ('xh', 'z', 'xl', 'yl'), 0, 0,...  29.9 us
    all_to_all x1, blocking collectives, per_device(): lax.all_to_all(spread.reshape(16, 4, half), AXES, 0, 0, axis_index_groups...  18 us
    pallas_call x1, Pallas kernels, per_device(): pl.pallas_call(tensor_kernel, out_shape=(piece, piece), in_specs=[VMEM, V...  3.9 us
  transfers between devices with their start and end apart: 1, of which 1 were waited for; matrix products, arithmetic and copies ran while one was open for 0% of the time, Pallas kernels for 0%

profile of v5, /device:TPU:4, one launch (start us, length us, event | category | flops | bytes accessed | tf_op | source)
XLA Modules:
  0.0 101.2 jit_solution(7463110846099619653)
XLA Ops:
  0.0 0.9 shard_map.28
  0.9 18.0 %all_to_all.15 = f32[16,4,1536]{2,1,0:T(4,128)S(1)} all-to-all(f32[16,4,1536]{2,1,0:T(4,128)S(1)} %bitcast.9), channel_id=1, replica_groups={{0,1,2,3,4,5,6,7,8,9,10,11,12,13,14,15},{16,17,18,19,20,21,22,23,24,25,..., dimensions={0} | all-to-all | bytes 786432 | tf_op jit(solution)/shard_map/all_to_all | solution.py:191
  18.8 0.2 shard_map.29
  19.1 43.7 %all_to_all.16.far_ref = f32[8,9,4,1536]{3,2,1,0:T(4,128)S(1)} all-to-all(f32[8,9,4,1536]{3,2,1,0:T(4,128)S(1)} %shard_map.29), channel_id=1, replica_groups={{0,16,32,48,64,80,96,112},{1,17,33,49,65,81,97,113},{2,18,34,50,66,82,9..., dimensions={0} | all-to-all | bytes 3538944 | tf_op jit(solution)/shard_map/all_to_all | solution.py:200
  62.8 3.9 %shard_map.30 = (f32[4,8,2,2,8,128]{5,4,3,2,1,0:T(8,128)S(1)}, f32[4,8,2,2,8,128]{5,4,3,2,1,0:T(8,128)S(1)}) custom-call(f32[2,8,4,1536]{3,2,1,0:T(4,128)S(1)} %bitcast.7, f32[8,9,4,1536]{3,2,1,0:T(4,128)S(1)} %all_to_all.16.far_ref), custom_call_target="tpu_custom_call" | custom-call | tf_op jit(solution)/shard_map/pallas_call | solution.py:202
  66.7 1.9 %collective-permute-start = (f32[4,8,2,2,8,128]{5,4,3,2,1,0:T(8,128)S(1)}, f32[4,8,2,2,8,128]{5,4,3,2,1,0:T(8,128)S(1)}, u32[]{:S(2)}, u32[]{:S(2)}) collective-permute-start(f32[4,8,2,2,8,128]{5,4,3,2,1,0:T(8,128)S(1)} %get-tuple-element.8), channel_id=1, source_target_pairs={{0,128},{128,0},{1,129},{129,1},{2,130},{130,2},{3,131},{131,3},{4... | collective-permute-start | bytes 1572872 | tf_op jit(solution)/shard_map/ppermute | solution.py:217
  68.6 1.9 %collective-permute-done = f32[4,8,2,2,8,128]{5,4,3,2,1,0:T(8,128)S(1)} collective-permute-done((f32[4,8,2,2,8,128]{5,4,3,2,1,0:T(8,128)S(1)}, f32[4,8,2,2,8,128]{5,4,3,2,1,0:T(8,128)S(1)}, u32[]{:S(2)}, u32[]{:S(2)}) %collective-permute-start) | collective-permute-done | bytes 524320 | tf_op jit(solution)/shard_map/ppermute | solution.py:217
  70.5 0.1 add.3
  70.6 29.9 %all_to_all.17 = f32[128,8,128]{2,1,0:T(8,128)S(1)} all-to-all(f32[128,8,128]{2,1,0:T(8,128)S(1)} %bitcast.10), channel_id=1, replica_groups=mesh['xh'=4,'core'=2,'z'=8,'xl'=2,'yh'=4,'yl'=2] {'xh','z','xl','yl'}, dimensions={0} | all-to-all | bytes 1048576 | tf_op jit(solution)/shard_map/all_to_all | solution.py:218
  100.5 0.8 shard_map.31
Async XLA Ops:
  66.7 3.8 %collective-permute-start = (f32[4,8,2,2,8,128]{5,4,3,2,1,0:T(8,128)S(1)}, f32[4,8,2,2,8,128]{5,4,3,2,1,0:T(8,128)S(1)}, u32[]{:S(2)}, u32[]{:S(2)}) collective-permute-start(f32[4,8,2,2,8,128]{5,4,3,2,1,0:T(8,128)S(1)} %get-tuple-element.8), channel_id=1, source_target_pairs={{0,128},{128,0},{1,129},{129,1},{2,130},{130,2},{3,131},{131,3},{4... | collective-permute-start | bytes 1572872 | tf_op jit(solution)/shard_map/ppermute | solution.py:217

commit v6 on v3

--- a/solution.py
+++ b/solution.py
@@ -9,9 +9,9 @@
 from jax.sharding import Mesh
 from jax.sharding import PartitionSpec as P
 
-AXES = ("xh", "core", "z", "xl", "yh", "yl")
+AXES = ("xh", "core", "zh", "zl", "xl", "yh", "yl")
 SPACE = ("xh", "core")
-MODES = ("z", "xl", "yh", "yl")
+MODES = ("zh", "zl", "xl", "yh", "yl")
 VMEM = pl.BlockSpec(memory_space=pltpu.VMEM)
 HBM = pl.BlockSpec(memory_space=pltpu.HBM)
 
@@ -43,37 +43,87 @@
 
 
 def pick_kernel(near_ref, out_ref):
-    yh, yl = lax.axis_index("yh"), lax.axis_index("yl")
-    for shard in range(5):
-        y = 2 * shard + yl if shard < 4 else 2 * yh + 1 - yl
+    core, yh, yl = lax.axis_index("core"), lax.axis_index("yh"), lax.axis_index("yl")
+    z = 2 * lax.axis_index("zh") + lax.axis_index("zl")
+
+    def put(piece, p, column):
         for xl in range(2):
-            piece = near_ref[xl, y, 0:2, :]
-            out_ref[shard, 2 * xl : 2 * xl + 2, :] = piece
-
-
-def tensor_kernel(near_ref, far_ref, keep_ref, send_ref, left, left2, mode_j, slope, prod_hi, prod_lo):
+            data = near_ref[xl, p, column : column + 2, :]
+            for peer in range(4):
+                out_ref[peer, piece, 2 * xl : 2 * xl + 2, :] = data
+
+    for piece in range(8):
+        y = 2 * piece + yl if piece < 4 else 2 * yh + 1 - yl
+        put(piece, jnp.where(core == 0, y, piece), 0)
+    put(8, z, 2)
+
+
+def pack_kernel(mid_ref, out_ref):
+    core, yh = lax.axis_index("core"), lax.axis_index("yh")
+    for zh in range(4):
+        for piece in range(5):
+            n = zh * 5 + piece
+            if n < 8:
+                first, second = yh, n
+            else:
+                first, second = (n - 8 if n < 12 else 0), 8
+            out_ref[n] = mid_ref[jnp.where(core == 0, zh, first), jnp.where(core == 0, piece, second)]
+
+
+def tensor_kernel(near_ref, mid_ref, got_ref, keep_ref, send_ref, left, left2, mode_j, slope, prod_hi, prod_lo):
     core, yh, yl = lax.axis_index("core"), lax.axis_index("yh"), lax.axis_index("yl")
-    for rel in range(2):
-        for xh in range(4):
-            z = 2 * xh + (core if rel == 0 else 1 - core)
+    zl = lax.axis_index("zl")
+
+    @pl.when(core == 0)
+    def _():
+        for other in range(2):
+            parity = 1 - zl if other else zl
+
+            def piece_of(zh, piece):
+                return got_ref[zh * 5 + piece] if other else mid_ref[zh, piece]
+
+            block = left.at[pl.ds(pl.multiple_of(parity * 64, 64), 64)]
+            for zh in range(4):
+                for q in range(4):
+                    row = zh * 16 + q * 4
+                    block[row : row + 4, :] = piece_of(zh, q)
+                modes = mode_j.at[pl.ds(pl.multiple_of(zh * 16 + parity * 8, 8), 8)]
+                for y in range(2):
+                    data = piece_of(zh, jnp.where(yl == y, yh, 4))
+                    for xl in range(2):
+                        row = xl * 4 + y * 2
+                        modes[row : row + 2, :] = data[2 * xl : 2 * xl + 2, :]
+        for xl in range(2):
+            for y in range(8):
+                row = xl * 16 + y * 2
+                slope[row : row + 2, :] = near_ref[xl, y, 2:4, :]
+
+    @pl.when(core != 0)
+    def _():
+        for z in range(8):
             for q in range(4):
-                row = rel * 64 + xh * 16 + q * 4
-                left[row : row + 4, :] = far_ref[z, q]
+                row = (1 - z % 2) * 64 + (z // 2) * 16 + q * 4
+                left[row : row + 4, :] = mid_ref[q, z]
+        for own in range(2):
+
+            @pl.when(yl == own)
+            def _():
+                for y in range(2):
+                    for z in range(8):
+                        data = mid_ref[yh, z] if y == own else got_ref[z]
+                        for xl in range(2):
+                            row = z * 8 + xl * 4 + y * 2
+                            mode_j[row : row + 2, :] = data[2 * xl : 2 * xl + 2, :]
+                    for q in range(4):
+                        data = mid_ref[q, 8] if y == own else got_ref[8 + q]
+                        for xl in range(2):
+                            row = xl * 16 + (2 * q + y) * 2
+                            slope[row : row + 2, :] = data[2 * xl : 2 * xl + 2, :]
+
     whole = left[...]
     high = whole.astype(jnp.bfloat16)
     left2[0:128, :] = high
     left2[128:256, :] = (whole - high.astype(jnp.float32)).astype(jnp.bfloat16)
-    for y in range(2):
-        shard = jnp.where(yl == y, yh, 4)
-        for z in range(8):
-            for xl in range(2):
-                row = z * 8 + xl * 4 + y * 2
-                mode_j[row : row + 2, :] = far_ref[z, shard, 2 * xl : 2 * xl + 2, :]
-    for xl in range(2):
-        for y in range(8):
-            row = xl * 16 + y * 2
-            slope[row : row + 2, :] = near_ref[xl, y, 2:4, :]
-
     lane = lax.broadcasted_iota(jnp.int32, (8, 128), 1)
     nt = (((1,), (1,)), ((), ()))
 
@@ -124,6 +174,26 @@
                         out_ref[i, bj : bj + 1, side * 128 : (side + 1) * 128] = wide[r : r + 1, :]
 
 
+def device(xh, core, z, xl, y):
+    return (((xh * 2 + core) * 8 + z) * 2 + xl) * 8 + y
+
+
+def gather_groups():
+    first, second, third = [], [], []
+    for xh in range(4):
+        for kept in range(8):
+            first.append([device(xh, 0, kept, xl, y) for xl in range(2) for y in range(8)])
+            first.append([device(xh, 1, z, xl, kept) for xl in range(2) for z in range(8)])
+            for xl in range(2):
+                for parity in range(2):
+                    second.append([device(xh, 0, parity + 2 * n, xl, kept) for n in range(4)])
+                    second.append([device(xh, 1, kept, xl, parity + 2 * n) for n in range(4)])
+                for n in range(8):
+                    third.append((device(xh, 0, n, xl, kept), device(xh, 0, n ^ 1, xl, kept)))
+                    third.append((device(xh, 1, kept, xl, n), device(xh, 1, kept, xl, n ^ 1)))
+    return first, second, third
+
+
 def per_device(modes_field, slopes):
     rows, own = modes_field.shape
     half = rows // 2
@@ -141,21 +211,30 @@
         ],
         compiler_params=room(8),
     )(in_place(modes_field.T), in_place(slopes.T))
-    near = lax.all_to_all(spread.reshape(16, 4, half), ("xl", "yh", "yl"), 0, 0, tiled=True)
+    first, second, third = gather_groups()
+    near = lax.all_to_all(spread.reshape(16, 4, half), AXES, 0, 0, axis_index_groups=first, tiled=True)
     near = on_chip(near.reshape(2, 8, 4, half))
     picked = pl.pallas_call(
         pick_kernel,
-        out_shape=pltpu.VMEM((5, 4, half), f32),
+        out_shape=pltpu.VMEM((4, 9, 4, half), f32),
         in_specs=[VMEM],
         out_specs=VMEM,
         compiler_params=room(8),
     )(near)
-    far = on_chip(lax.all_gather(picked, "z", axis=0))
+    mid = on_chip(lax.all_to_all(picked, AXES, 0, 0, axis_index_groups=second, tiled=True))
+    packed = pl.pallas_call(
+        pack_kernel,
+        out_shape=pltpu.VMEM((20, 4, half), f32),
+        in_specs=[VMEM],
+        out_specs=VMEM,
+        compiler_params=room(8),
+    )(mid)
+    got = on_chip(lax.ppermute(packed, AXES, third))
     piece = pltpu.VMEM((4, 8, 2, 2, 8, 128), f32)
     keep, send = pl.pallas_call(
         tensor_kernel,
         out_shape=(piece, piece),
-        in_specs=[VMEM, VMEM],
+        in_specs=[VMEM, VMEM, VMEM],
         out_specs=(VMEM, VMEM),
         scratch_shapes=[
             pltpu.VMEM((128, half), f32),
@@ -166,9 +245,9 @@
             pltpu.VMEM((2, 1024, half), jnp.bfloat16),
         ],
         compiler_params=room(24),
-    )(near, far)
+    )(near, mid, got)
     pair = keep + lax.ppermute(send, "core", [(0, 1), (1, 0)])
-    parts = lax.all_to_all(pair.reshape(128, 8, 128), ("xh", "z", "xl", "yl"), 0, 0, tiled=True)
+    parts = lax.all_to_all(pair.reshape(128, 8, 128), ("xh", "zh", "zl", "xl", "yl"), 0, 0, tiled=True)
     return pl.pallas_call(
         functools.partial(finish_kernel, factor),
         out_shape=jax.ShapeDtypeStruct((32, 2, 256), f32),
@@ -179,7 +258,7 @@
 
 
 def solution(mesh):
-    fine = Mesh(mesh.devices.reshape(4, 2, 8, 2, 4, 2), AXES)
+    fine = Mesh(mesh.devices.reshape(4, 2, 4, 2, 2, 4, 2), AXES)
     placed = P(SPACE, MODES)
     return jax.shard_map(
         per_device, mesh=fine, in_specs=(placed, placed), out_specs=P(SPACE, MODES, None), check_vma=False

time: 102 us -> 102 us (level)
  blocking collectives: 92.4 us -> 81.4 us
  waiting for transfers between devices: 1.88 us -> 10.1 us
  starting transfers between devices: 1.92 us -> 4.4 us
    all_gather x1 -> x0, blocking collectives: 39.4 us -> none  [per_device(): far = on_chip(lax.all_gather(picked, 'z', axis=0))]
    all_to_all x2 -> x3, blocking collectives: 53 us -> 81.4 us  [the longest x1 33.3 us: per_device(): lax.all_to_all(picked, AXES, 0, 0, axis_index_groups=second, tiled=True)]
    ppermute x0 -> x1, waiting for transfers between devices: none -> 8.23 us  [per_device(): got = on_chip(lax.ppermute(packed, AXES, third))]
    ppermute x0 -> x1, starting transfers between devices: none -> 2.48 us  [per_device(): got = on_chip(lax.ppermute(packed, AXES, third))]
  transfers between devices with their start and end apart: 1 -> 2, of which waited for: 1 -> 2; matrix products, arithmetic and copies ran while one was open for 0% -> 0% of each run, Pallas kernels for 0% -> 0%
where the time goes in v6:
time: 102 us
  blocking collectives  81.4 us (80%)
  waiting for transfers between devices  10.1 us (10%)
  Pallas kernels  5.7 us (6%)
  starting transfers between devices  4.4 us (4%)
    all_to_all x1, blocking collectives, per_device(): lax.all_to_all(picked, AXES, 0, 0, axis_index_groups=second, tiled=True)  33.3 us
    all_to_all x1, blocking collectives, per_device(): lax.all_to_all(pair.reshape(128, 8, 128), ('xh', 'zh', 'zl', 'xl', 'yl'),...  30.1 us
    all_to_all x1, blocking collectives, per_device(): lax.all_to_all(spread.reshape(16, 4, half), AXES, 0, 0, axis_index_groups...  18 us
    ppermute x1, waiting for transfers between devices, per_device(): got = on_chip(lax.ppermute(packed, AXES, third))  8.23 us
    pallas_call x1, Pallas kernels, per_device(): pl.pallas_call(tensor_kernel, out_shape=(piece, piece), in_specs=[VMEM, V...  3.9 us
    ppermute x1, starting transfers between devices, per_device(): got = on_chip(lax.ppermute(packed, AXES, third))  2.48 us
  transfers between devices with their start and end apart: 2, of which 2 were waited for; matrix products, arithmetic and copies ran while one was open for 0% of the time, Pallas kernels for 0%

profile of v6, /device:TPU:4, one launch (start us, length us, event | category | flops | bytes accessed | tf_op | source)
XLA Modules:
  0.0 101.8 jit_solution(1331898386749845542)
XLA Ops:
  0.0 0.9 shard_map.28
  0.9 18.0 %all_to_all.15 = f32[16,4,1536]{2,1,0:T(4,128)S(1)} all-to-all(f32[16,4,1536]{2,1,0:T(4,128)S(1)} %bitcast.9), channel_id=1, replica_groups={{0,1,2,3,4,5,6,7,8,9,10,11,12,13,14,15},{128,144,160,176,192,208,224,24..., dimensions={0} | all-to-all | bytes 786432 | tf_op jit(solution)/shard_map/all_to_all | solution.py:215
  18.8 0.1 shard_map.29
  19.0 33.3 %all_to_all.16.mid_ref = f32[4,9,4,1536]{3,2,1,0:T(4,128)S(1)} all-to-all(f32[4,9,4,1536]{3,2,1,0:T(4,128)S(1)} %shard_map.29), channel_id=1, replica_groups={{0,32,64,96},{128,130,132,134},{16,48,80,112},{129,131,133,135},{8,40,7..., dimensions={0} | all-to-all | bytes 1769472 | tf_op jit(solution)/shard_map/all_to_all | solution.py:224
  52.3 2.5 %collective-permute-start = (f32[20,4,1536]{2,1,0:T(4,128)S(1)}, f32[20,4,1536]{2,1,0:T(4,128)S(1)}, u32[]{:S(2)}, u32[]{:S(2)}) collective-permute-start(f32[20,4,1536]{2,1,0:T(4,128)S(1)} %shard_map.30), channel_id=1, source_target_pairs={{0,16},{128,129},{16,0},{129,128},{32,48},{130,131},{48,32},{131,1... | collective-permute-start | bytes 1474568 | tf_op jit(solution)/shard_map/ppermute | solution.py:232
  54.8 8.2 %collective-permute-done.got_ref = f32[20,4,1536]{2,1,0:T(4,128)S(1)} collective-permute-done((f32[20,4,1536]{2,1,0:T(4,128)S(1)}, f32[20,4,1536]{2,1,0:T(4,128)S(1)}, u32[]{:S(2)}, u32[]{:S(2)}) %collective-permute-start) | collective-permute-done | bytes 491552 | tf_op jit(solution)/shard_map/ppermute | solution.py:232
  63.0 3.9 %shard_map.31 = (f32[4,8,2,2,8,128]{5,4,3,2,1,0:T(8,128)S(1)}, f32[4,8,2,2,8,128]{5,4,3,2,1,0:T(8,128)S(1)}) custom-call(f32[2,8,4,1536]{3,2,1,0:T(4,128)S(1)} %bitcast.7, f32[4,9,4,1536]{3,2,1,0:T(4,128)S(1)} %all_to_all.16.mid_ref, f32[20,4,1536]{2,1,0:T(4,128)S(1)} %collective-permute-done.got_ref), custom_call_target="tpu_custom_call" | custom-call | tf_op jit(solution)/shard_map/pallas_call | solution.py:234
  67.0 1.9 %collective-permute-start.1 = (f32[4,8,2,2,8,128]{5,4,3,2,1,0:T(8,128)S(1)}, f32[4,8,2,2,8,128]{5,4,3,2,1,0:T(8,128)S(1)}, u32[]{:S(2)}, u32[]{:S(2)}) collective-permute-start(f32[4,8,2,2,8,128]{5,4,3,2,1,0:T(8,128)S(1)} %get-tuple-element.8), channel_id=1, source_target_pairs={{0,128},{128,0},{1,129},{129,1},{2,130},{130,2},{3,131},{131,3},{4... | collective-permute-start | bytes 1572872 | tf_op jit(solution)/shard_map/ppermute | solution.py:249
  68.9 1.9 %collective-permute-done.1 = f32[4,8,2,2,8,128]{5,4,3,2,1,0:T(8,128)S(1)} collective-permute-done((f32[4,8,2,2,8,128]{5,4,3,2,1,0:T(8,128)S(1)}, f32[4,8,2,2,8,128]{5,4,3,2,1,0:T(8,128)S(1)}, u32[]{:S(2)}, u32[]{:S(2)}) %collective-permute-start.1) | collective-permute-done | bytes 524320 | tf_op jit(solution)/shard_map/ppermute | solution.py:249
  70.8 0.1 add.3
  70.9 30.1 %all_to_all.17 = f32[128,8,128]{2,1,0:T(8,128)S(1)} all-to-all(f32[128,8,128]{2,1,0:T(8,128)S(1)} %bitcast.10), channel_id=1, replica_groups=mesh['xh'=4,'core'=2,'zh'=4,'zl'=2,'xl'=2,'yh'=4,'yl'=2] {'xh','zh','zl'..., dimensions={0} | all-to-all | bytes 1048576 | tf_op jit(solution)/shard_map/all_to_all | solution.py:250
  101.0 0.8 shard_map.32
  (1 shorter events, 0.0 us)
Async XLA Ops:
  52.3 10.7 %collective-permute-start = (f32[20,4,1536]{2,1,0:T(4,128)S(1)}, f32[20,4,1536]{2,1,0:T(4,128)S(1)}, u32[]{:S(2)}, u32[]{:S(2)}) collective-permute-start(f32[20,4,1536]{2,1,0:T(4,128)S(1)} %shard_map.30), channel_id=1, source_target_pairs={{0,16},{128,129},{16,0},{129,128},{32,48},{130,131},{48,32},{131,1... | collective-permute-start | bytes 1474568 | tf_op jit(solution)/shard_map/ppermute | solution.py:232
  67.0 3.8 %collective-permute-start.1 = (f32[4,8,2,2,8,128]{5,4,3,2,1,0:T(8,128)S(1)}, f32[4,8,2,2,8,128]{5,4,3,2,1,0:T(8,128)S(1)}, u32[]{:S(2)}, u32[]{:S(2)}) collective-permute-start(f32[4,8,2,2,8,128]{5,4,3,2,1,0:T(8,128)S(1)} %get-tuple-element.8), channel_id=1, source_target_pairs={{0,128},{128,0},{1,129},{129,1},{2,130},{130,2},{3,131},{131,3},{4... | collective-permute-start | bytes 1572872 | tf_op jit(solution)/shard_map/ppermute | solution.py:249

commit v7 on v6

--- a/solution.py
+++ b/solution.py
@@ -58,19 +58,20 @@
     put(8, z, 2)
 
 
-def pack_kernel(mid_ref, out_ref):
-    core, yh = lax.axis_index("core"), lax.axis_index("yh")
-    for zh in range(4):
-        for piece in range(5):
-            n = zh * 5 + piece
-            if n < 8:
-                first, second = yh, n
+def pack_kernel(mid_ref, up_ref, down_ref):
+    core, yh, yl = lax.axis_index("core"), lax.axis_index("yh"), lax.axis_index("yl")
+    for half, out_ref in ((0, up_ref), (1, down_ref)):
+        theirs = lax.rem(yh + yl + (4 if half == 0 else 3), 4)
+        for n in range(10):
+            if n < 4:
+                first, second = theirs, 4 * half + n
             else:
-                first, second = (n - 8 if n < 12 else 0), 8
+                first, second = 2 * half + n % 2, 8
+            zh, piece = 2 * half + n // 5, n % 5
             out_ref[n] = mid_ref[jnp.where(core == 0, zh, first), jnp.where(core == 0, piece, second)]
 
 
-def tensor_kernel(near_ref, mid_ref, got_ref, keep_ref, send_ref, left, left2, mode_j, slope, prod_hi, prod_lo):
+def tensor_kernel(near_ref, mid_ref, below_ref, above_ref, keep_ref, send_ref, left, left2, mode_j, slope, prod_hi, prod_lo):
     core, yh, yl = lax.axis_index("core"), lax.axis_index("yh"), lax.axis_index("yl")
     zl = lax.axis_index("zl")
 
@@ -80,7 +81,9 @@
             parity = 1 - zl if other else zl
 
             def piece_of(zh, piece):
-                return got_ref[zh * 5 + piece] if other else mid_ref[zh, piece]
+                if not other:
+                    return mid_ref[zh, piece]
+                return (below_ref if zh < 2 else above_ref)[zh % 2 * 5 + piece]
 
             block = left.at[pl.ds(pl.multiple_of(parity * 64, 64), 64)]
             for zh in range(4):
@@ -110,12 +113,12 @@
             def _():
                 for y in range(2):
                     for z in range(8):
-                        data = mid_ref[yh, z] if y == own else got_ref[z]
+                        data = mid_ref[yh, z] if y == own else (below_ref if z < 4 else above_ref)[z % 4]
                         for xl in range(2):
                             row = z * 8 + xl * 4 + y * 2
                             mode_j[row : row + 2, :] = data[2 * xl : 2 * xl + 2, :]
                     for q in range(4):
-                        data = mid_ref[q, 8] if y == own else got_ref[8 + q]
+                        data = mid_ref[q, 8] if y == own else (below_ref if q < 2 else above_ref)[4 + q % 2]
                         for xl in range(2):
                             row = xl * 16 + (2 * q + y) * 2
                             slope[row : row + 2, :] = data[2 * xl : 2 * xl + 2, :]
@@ -189,8 +192,8 @@
                     second.append([device(xh, 0, parity + 2 * n, xl, kept) for n in range(4)])
                     second.append([device(xh, 1, kept, xl, parity + 2 * n) for n in range(4)])
                 for n in range(8):
-                    third.append((device(xh, 0, n, xl, kept), device(xh, 0, n ^ 1, xl, kept)))
-                    third.append((device(xh, 1, kept, xl, n), device(xh, 1, kept, xl, n ^ 1)))
+                    third.append((device(xh, 0, n, xl, kept), device(xh, 0, (n + 1) % 8, xl, kept)))
+                    third.append((device(xh, 1, kept, xl, n), device(xh, 1, kept, xl, (n + 1) % 8)))
     return first, second, third
 
 
@@ -222,19 +225,21 @@
         compiler_params=room(8),
     )(near)
     mid = on_chip(lax.all_to_all(picked, AXES, 0, 0, axis_index_groups=second, tiled=True))
-    packed = pl.pallas_call(
+    ten = pltpu.VMEM((10, 4, half), f32)
+    up, down = pl.pallas_call(
         pack_kernel,
-        out_shape=pltpu.VMEM((20, 4, half), f32),
+        out_shape=(ten, ten),
         in_specs=[VMEM],
-        out_specs=VMEM,
+        out_specs=(VMEM, VMEM),
         compiler_params=room(8),
     )(mid)
-    got = on_chip(lax.ppermute(packed, AXES, third))
+    below = on_chip(lax.ppermute(up, AXES, third))
+    above = on_chip(lax.ppermute(down, AXES, [(b, a) for a, b in third]))
     piece = pltpu.VMEM((4, 8, 2, 2, 8, 128), f32)
     keep, send = pl.pallas_call(
         tensor_kernel,
         out_shape=(piece, piece),
-        in_specs=[VMEM, VMEM, VMEM],
+        in_specs=[VMEM] * 4,
         out_specs=(VMEM, VMEM),
         scratch_shapes=[
             pltpu.VMEM((128, half), f32),
@@ -245,7 +250,7 @@
             pltpu.VMEM((2, 1024, half), jnp.bfloat16),
         ],
         compiler_params=room(24),
-    )(near, mid, got)
+    )(near, mid, below, above)
     pair = keep + lax.ppermute(send, "core", [(0, 1), (1, 0)])
     parts = lax.all_to_all(pair.reshape(128, 8, 128), ("xh", "zh", "zl", "xl", "yl"), 0, 0, tiled=True)
     return pl.pallas_call(

time: 102 us -> 104 us (1.020)
  starting transfers between devices: 4.4 us -> 8.97 us
  waiting for transfers between devices: 10.1 us -> 5.57 us
  blocking collectives: 81.4 us -> 83.7 us
    ppermute x1 -> x2, starting transfers between devices: 2.48 us -> 7.05 us  [the longest x1 4.57 us: per_device(): above = on_chip(lax.ppermute(down, AXES, [(b, a) for a, b in third]))]
    ppermute x1 -> x2, waiting for transfers between devices: 8.23 us -> 3.69 us  [the longest x1 2.23 us: per_device(): below = on_chip(lax.ppermute(up, AXES, third))]
    all_to_all x1, blocking collectives: 30.1 us -> 32.4 us  [per_device(): lax.all_to_all(pair.reshape(128, 8, 128), ('xh', 'zh', 'zl', 'xl', 'yl'),...]
  transfers between devices with their start and end apart: 2 -> 3, of which waited for: 2 -> 3; matrix products, arithmetic and copies ran while one was open for 0% -> 0% of each run, Pallas kernels for 0% -> 0%
where the time goes in v7:
time: 104 us
  blocking collectives  83.7 us (80%)
  starting transfers between devices  8.97 us (9%)
  Pallas kernels  5.7 us (5%)
  waiting for transfers between devices  5.57 us (5%)
    all_to_all x1, blocking collectives, per_device(): lax.all_to_all(picked, AXES, 0, 0, axis_index_groups=second, tiled=True)  33.3 us
    all_to_all x1, blocking collectives, per_device(): lax.all_to_all(pair.reshape(128, 8, 128), ('xh', 'zh', 'zl', 'xl', 'yl'),...  32.4 us
    all_to_all x1, blocking collectives, per_device(): lax.all_to_all(spread.reshape(16, 4, half), AXES, 0, 0, axis_index_groups...  18 us
    ppermute x1, starting transfers between devices, per_device(): above = on_chip(lax.ppermute(down, AXES, [(b, a) for a, b in third]))  4.57 us
    pallas_call x1, Pallas kernels, per_device(): pl.pallas_call(tensor_kernel, out_shape=(piece, piece), in_specs=[VMEM] *...  3.91 us
    ppermute x1, starting transfers between devices, per_device(): below = on_chip(lax.ppermute(up, AXES, third))  2.48 us
    ppermute x1, waiting for transfers between devices, per_device(): below = on_chip(lax.ppermute(up, AXES, third))  2.23 us
  transfers between devices with their start and end apart: 3, of which 3 were waited for; matrix products, arithmetic and copies ran while one was open for 0% of the time, Pallas kernels for 0%

profile of v7, /device:TPU:4, one launch (start us, length us, event | category | flops | bytes accessed | tf_op | source)
XLA Modules:
  0.0 104.0 jit_solution(12968466443293178886)
XLA Ops:
  0.0 0.9 shard_map.28
  0.9 18.0 %all_to_all.15 = f32[16,4,1536]{2,1,0:T(4,128)S(1)} all-to-all(f32[16,4,1536]{2,1,0:T(4,128)S(1)} %bitcast.9), channel_id=1, replica_groups={{0,1,2,3,4,5,6,7,8,9,10,11,12,13,14,15},{128,144,160,176,192,208,224,24..., dimensions={0} | all-to-all | bytes 786432 | tf_op jit(solution)/shard_map/all_to_all | solution.py:218
  18.8 0.1 shard_map.29
  19.0 33.3 %all_to_all.16.mid_ref = f32[4,9,4,1536]{3,2,1,0:T(4,128)S(1)} all-to-all(f32[4,9,4,1536]{3,2,1,0:T(4,128)S(1)} %shard_map.29), channel_id=1, replica_groups={{0,32,64,96},{128,130,132,134},{16,48,80,112},{129,131,133,135},{8,40,7..., dimensions={0} | all-to-all | bytes 1769472 | tf_op jit(solution)/shard_map/all_to_all | solution.py:227
  52.3 2.5 %collective-permute-start = (f32[10,4,1536]{2,1,0:T(4,128)S(1)}, f32[10,4,1536]{2,1,0:T(4,128)S(1)}, u32[]{:S(2)}, u32[]{:S(2)}) collective-permute-start(f32[10,4,1536]{2,1,0:T(4,128)S(1)} %get-tuple-element.9), channel_id=1, source_target_pairs={{0,16},{128,129},{16,32},{129,130},{32,48},{130,131},{48,64},{131,... | collective-permute-start | bytes 737288 | tf_op jit(solution)/shard_map/ppermute | solution.py:236
  54.8 4.6 %collective-permute-start.1 = (f32[10,4,1536]{2,1,0:T(4,128)S(1)}, f32[10,4,1536]{2,1,0:T(4,128)S(1)}, u32[]{:S(2)}, u32[]{:S(2)}) collective-permute-start(f32[10,4,1536]{2,1,0:T(4,128)S(1)} %get-tuple-element.10), channel_id=1, source_target_pairs={{16,0},{129,128},{32,16},{130,129},{48,32},{131,130},{64,48},{132,... | collective-permute-start | bytes 737288 | tf_op jit(solution)/shard_map/ppermute | solution.py:237
  59.4 2.2 %collective-permute-done.below_ref = f32[10,4,1536]{2,1,0:T(4,128)S(1)} collective-permute-done((f32[10,4,1536]{2,1,0:T(4,128)S(1)}, f32[10,4,1536]{2,1,0:T(4,128)S(1)}, u32[]{:S(2)}, u32[]{:S(2)}) %collective-permute-start) | collective-permute-done | bytes 245792 | tf_op jit(solution)/shard_map/ppermute | solution.py:236
  61.6 1.5 %collective-permute-done.1.above_ref = f32[10,4,1536]{2,1,0:T(4,128)S(1)} collective-permute-done((f32[10,4,1536]{2,1,0:T(4,128)S(1)}, f32[10,4,1536]{2,1,0:T(4,128)S(1)}, u32[]{:S(2)}, u32[]{:S(2)}) %collective-permute-start.1) | collective-permute-done | bytes 245792 | tf_op jit(solution)/shard_map/ppermute | solution.py:237
  63.1 3.9 %shard_map.31 = (f32[4,8,2,2,8,128]{5,4,3,2,1,0:T(8,128)S(1)}, f32[4,8,2,2,8,128]{5,4,3,2,1,0:T(8,128)S(1)}) custom-call(f32[2,8,4,1536]{3,2,1,0:T(4,128)S(1)} %bitcast.7, f32[4,9,4,1536]{3,2,1,0:T(4,128)S(1)} %all_to_all.16.mid_ref, f32[10,4,1536]{2,1,0:T(4,128)S(1)} %collective-permute-done.below_ref, f32[10,4,1536]{2,1,0:T(4,128)S(1)} %collective-permute-done.1.above_ref), custom_call_target="tpu_custom_call" | custom-call | tf_op jit(solution)/shard_map/pallas_call | solution.py:239
  67.0 1.9 %collective-permute-start.2 = (f32[4,8,2,2,8,128]{5,4,3,2,1,0:T(8,128)S(1)}, f32[4,8,2,2,8,128]{5,4,3,2,1,0:T(8,128)S(1)}, u32[]{:S(2)}, u32[]{:S(2)}) collective-permute-start(f32[4,8,2,2,8,128]{5,4,3,2,1,0:T(8,128)S(1)} %get-tuple-element.12), channel_id=1, source_target_pairs={{0,128},{128,0},{1,129},{129,1},{2,130},{130,2},{3,131},{131,3},{4... | collective-permute-start | bytes 1572872 | tf_op jit(solution)/shard_map/ppermute | solution.py:254
  68.9 1.9 %collective-permute-done.2 = f32[4,8,2,2,8,128]{5,4,3,2,1,0:T(8,128)S(1)} collective-permute-done((f32[4,8,2,2,8,128]{5,4,3,2,1,0:T(8,128)S(1)}, f32[4,8,2,2,8,128]{5,4,3,2,1,0:T(8,128)S(1)}, u32[]{:S(2)}, u32[]{:S(2)}) %collective-permute-start.2) | collective-permute-done | bytes 524320 | tf_op jit(solution)/shard_map/ppermute | solution.py:254
  70.8 0.1 add.3
  70.9 32.4 %all_to_all.17 = f32[128,8,128]{2,1,0:T(8,128)S(1)} all-to-all(f32[128,8,128]{2,1,0:T(8,128)S(1)} %bitcast.10), channel_id=1, replica_groups=mesh['xh'=4,'core'=2,'zh'=4,'zl'=2,'xl'=2,'yh'=4,'yl'=2] {'xh','zh','zl'..., dimensions={0} | all-to-all | bytes 1048576 | tf_op jit(solution)/shard_map/all_to_all | solution.py:255
  103.3 0.8 shard_map.32
  (1 shorter events, 0.0 us)
Async XLA Ops:
  52.3 9.3 %collective-permute-start = (f32[10,4,1536]{2,1,0:T(4,128)S(1)}, f32[10,4,1536]{2,1,0:T(4,128)S(1)}, u32[]{:S(2)}, u32[]{:S(2)}) collective-permute-start(f32[10,4,1536]{2,1,0:T(4,128)S(1)} %get-tuple-element.9), channel_id=1, source_target_pairs={{0,16},{128,129},{16,32},{129,130},{32,48},{130,131},{48,64},{131,... | collective-permute-start | bytes 737288 | tf_op jit(solution)/shard_map/ppermute | solution.py:236
  54.8 8.3 %collective-permute-start.1 = (f32[10,4,1536]{2,1,0:T(4,128)S(1)}, f32[10,4,1536]{2,1,0:T(4,128)S(1)}, u32[]{:S(2)}, u32[]{:S(2)}) collective-permute-start(f32[10,4,1536]{2,1,0:T(4,128)S(1)} %get-tuple-element.10), channel_id=1, source_target_pairs={{16,0},{129,128},{32,16},{130,129},{48,32},{131,130},{64,48},{132,... | collective-permute-start | bytes 737288 | tf_op jit(solution)/shard_map/ppermute | solution.py:237
  67.0 3.8 %collective-permute-start.2 = (f32[4,8,2,2,8,128]{5,4,3,2,1,0:T(8,128)S(1)}, f32[4,8,2,2,8,128]{5,4,3,2,1,0:T(8,128)S(1)}, u32[]{:S(2)}, u32[]{:S(2)}) collective-permute-start(f32[4,8,2,2,8,128]{5,4,3,2,1,0:T(8,128)S(1)} %get-tuple-element.12), channel_id=1, source_target_pairs={{0,128},{128,0},{1,129},{129,1},{2,130},{130,2},{3,131},{131,3},{4... | collective-permute-start | bytes 1572872 | tf_op jit(solution)/shard_map/ppermute | solution.py:254

commit v8 on v5

--- a/solution.py
+++ b/solution.py
@@ -116,8 +116,8 @@
             for s in range(8):
                 ref, xh = (keep_ref, s) if s < 4 else (send_ref, s - 4)
                 top, low = tile[s * 16 : s * 16 + 8, :], tile[s * 16 + 8 : s * 16 + 16, :]
-                ref[xh, z, xl, 0] = jnp.where(lane < 64, top, pltpu.roll(low, 64, 1))
-                ref[xh, z, xl, 1] = jnp.where(lane < 64, pltpu.roll(top, 64, 1), low)
+                ref[0, xl, z, xh] = jnp.where(lane < 64, top, pltpu.roll(low, 64, 1))
+                ref[1, xl, z, xh] = jnp.where(lane < 64, pltpu.roll(top, 64, 1), low)
 
 
 def finish_kernel(factor, parts_ref, out_ref):
@@ -125,11 +125,11 @@
     for yl in range(2):
         sums = []
         for z in range(8):
-            total = parts_ref[0, z, 0, yl]
+            total = parts_ref[yl, 0, z, 0]
             for xh in range(4):
                 for xl in range(2):
                     if xh or xl:
-                        total = total + parts_ref[xh, z, xl, yl]
+                        total = total + parts_ref[yl, xl, z, xh]
             sums.append(total * factor)
         for h in range(2):
             for bj in range(2):
@@ -168,6 +168,20 @@
                         line.append((((xh * 2 + core) * 8 + z) * 2 + xl) * 8 + y)
                     second.append(line)
     return first, second
+
+
+def owner_groups():
+    return [
+        [
+            (((xh * 2 + core) * 8 + z) * 2 + xl) * 8 + yh * 2 + yl
+            for yl in range(2)
+            for xl in range(2)
+            for z in range(8)
+            for xh in range(4)
+        ]
+        for core in range(2)
+        for yh in range(4)
+    ]
 
 
 def per_device(modes_field, slopes):
@@ -198,7 +212,7 @@
         compiler_params=room(8),
     )(near)
     far = on_chip(lax.all_to_all(picked, AXES, 0, 0, axis_index_groups=second, tiled=True))
-    piece = pltpu.VMEM((4, 8, 2, 2, 8, 128), f32)
+    piece = pltpu.VMEM((2, 2, 8, 4, 8, 128), f32)
     keep, send = pl.pallas_call(
         tensor_kernel,
         out_shape=(piece, piece),
@@ -215,14 +229,14 @@
         compiler_params=room(24),
     )(near, far)
     pair = keep + lax.ppermute(send, "core", [(0, 1), (1, 0)])
-    parts = lax.all_to_all(pair.reshape(128, 8, 128), ("xh", "z", "xl", "yl"), 0, 0, tiled=True)
+    parts = lax.all_to_all(pair.reshape(128, 8, 128), AXES, 0, 0, axis_index_groups=owner_groups(), tiled=True)
     return pl.pallas_call(
         functools.partial(finish_kernel, factor),
         out_shape=jax.ShapeDtypeStruct((32, 2, 256), f32),
         in_specs=[VMEM],
         out_specs=VMEM,
         compiler_params=room(8),
-    )(on_chip(parts.reshape(4, 8, 2, 2, 8, 128)))
+    )(on_chip(parts.reshape(2, 2, 8, 4, 8, 128)))
 
 
 def solution(mesh):

time: 102 us -> 102 us (level)
  the two profiles are of different devices: /device:TPU:4 before, /device:TPU:2 now
where the time goes in v8:
time: 102 us
  blocking collectives  92 us (90%)
  Pallas kernels  5.77 us (6%)
  starting transfers between devices  1.92 us (2%)
  waiting for transfers between devices  1.88 us (2%)
    all_to_all x1, blocking collectives, per_device(): lax.all_to_all(picked, AXES, 0, 0, axis_index_groups=second, tiled=True)  36.3 us
    all_to_all x1, blocking collectives, per_device(): lax.all_to_all(pair.reshape(128, 8, 128), AXES, 0, 0, axis_index_groups=o...  31.3 us
    all_to_all x1, blocking collectives, per_device(): lax.all_to_all(spread.reshape(16, 4, half), AXES, 0, 0, axis_index_groups...  24.4 us
    pallas_call x1, Pallas kernels, per_device(): pl.pallas_call(tensor_kernel, out_shape=(piece, piece), in_specs=[VMEM, V...  3.9 us
  transfers between devices with their start and end apart: 1, of which 1 were waited for; matrix products, arithmetic and copies ran while one was open for 0% of the time, Pallas kernels for 0%

profile of v8, /device:TPU:2, one launch (start us, length us, event | category | flops | bytes accessed | tf_op | source)
XLA Modules:
  0.0 101.7 jit_solution(15790621008476710142)
XLA Ops:
  0.0 0.9 shard_map.28
  0.9 24.4 %all_to_all.15 = f32[16,4,1536]{2,1,0:T(4,128)S(1)} all-to-all(f32[16,4,1536]{2,1,0:T(4,128)S(1)} %bitcast.9), channel_id=1, replica_groups={{0,1,2,3,4,5,6,7,8,9,10,11,12,13,14,15},{16,17,18,19,20,21,22,23,24,25,..., dimensions={0} | all-to-all | bytes 786432 | tf_op jit(solution)/shard_map/all_to_all | solution.py:205
  25.3 0.2 shard_map.29
  25.5 36.3 %all_to_all.16.far_ref = f32[8,9,4,1536]{3,2,1,0:T(4,128)S(1)} all-to-all(f32[8,9,4,1536]{3,2,1,0:T(4,128)S(1)} %shard_map.29), channel_id=1, replica_groups={{0,16,32,48,64,80,96,112},{1,17,33,49,65,81,97,113},{2,18,34,50,66,82,9..., dimensions={0} | all-to-all | bytes 3538944 | tf_op jit(solution)/shard_map/all_to_all | solution.py:214
  61.8 3.9 %shard_map.30 = (f32[2,2,8,4,8,128]{5,4,3,2,1,0:T(8,128)S(1)}, f32[2,2,8,4,8,128]{5,4,3,2,1,0:T(8,128)S(1)}) custom-call(f32[2,8,4,1536]{3,2,1,0:T(4,128)S(1)} %bitcast.7, f32[8,9,4,1536]{3,2,1,0:T(4,128)S(1)} %all_to_all.16.far_ref), custom_call_target="tpu_custom_call" | custom-call | tf_op jit(solution)/shard_map/pallas_call | solution.py:216
  65.7 1.9 %collective-permute-start = (f32[2,2,8,4,8,128]{5,4,3,2,1,0:T(8,128)S(1)}, f32[2,2,8,4,8,128]{5,4,3,2,1,0:T(8,128)S(1)}, u32[]{:S(2)}, u32[]{:S(2)}) collective-permute-start(f32[2,2,8,4,8,128]{5,4,3,2,1,0:T(8,128)S(1)} %get-tuple-element.8), channel_id=1, source_target_pairs={{0,128},{128,0},{1,129},{129,1},{2,130},{130,2},{3,131},{131,3},{4... | collective-permute-start | bytes 1572872 | tf_op jit(solution)/shard_map/ppermute | solution.py:231
  67.6 1.9 %collective-permute-done = f32[2,2,8,4,8,128]{5,4,3,2,1,0:T(8,128)S(1)} collective-permute-done((f32[2,2,8,4,8,128]{5,4,3,2,1,0:T(8,128)S(1)}, f32[2,2,8,4,8,128]{5,4,3,2,1,0:T(8,128)S(1)}, u32[]{:S(2)}, u32[]{:S(2)}) %collective-permute-start) | collective-permute-done | bytes 524320 | tf_op jit(solution)/shard_map/ppermute | solution.py:231
  69.5 0.1 add.3
  69.6 31.3 %all_to_all.17 = f32[128,8,128]{2,1,0:T(8,128)S(1)} all-to-all(f32[128,8,128]{2,1,0:T(8,128)S(1)} %bitcast.10), channel_id=1, replica_groups={{0,256,512,768,16,272,528,784,32,288,544,800,48,304,560,816,64,320,576,..., dimensions={0} | all-to-all | bytes 1048576 | tf_op jit(solution)/shard_map/all_to_all | solution.py:232
  100.9 0.8 shard_map.31
Async XLA Ops:
  65.7 3.8 %collective-permute-start = (f32[2,2,8,4,8,128]{5,4,3,2,1,0:T(8,128)S(1)}, f32[2,2,8,4,8,128]{5,4,3,2,1,0:T(8,128)S(1)}, u32[]{:S(2)}, u32[]{:S(2)}) collective-permute-start(f32[2,2,8,4,8,128]{5,4,3,2,1,0:T(8,128)S(1)} %get-tuple-element.8), channel_id=1, source_target_pairs={{0,128},{128,0},{1,129},{129,1},{2,130},{130,2},{3,131},{131,3},{4... | collective-permute-start | bytes 1572872 | tf_op jit(solution)/shard_map/ppermute | solution.py:231

commit v9 on v6

--- a/solution.py
+++ b/solution.py
@@ -60,6 +60,7 @@
 
 def pack_kernel(mid_ref, out_ref):
     core, yh = lax.axis_index("core"), lax.axis_index("yh")
+    other = 1 - jnp.where(core == 0, lax.axis_index("zl"), lax.axis_index("yl"))
     for zh in range(4):
         for piece in range(5):
             n = zh * 5 + piece
@@ -67,7 +68,7 @@
                 first, second = yh, n
             else:
                 first, second = (n - 8 if n < 12 else 0), 8
-            out_ref[n] = mid_ref[jnp.where(core == 0, zh, first), jnp.where(core == 0, piece, second)]
+            out_ref[other, n] = mid_ref[jnp.where(core == 0, zh, first), jnp.where(core == 0, piece, second)]
 
 
 def tensor_kernel(near_ref, mid_ref, got_ref, keep_ref, send_ref, left, left2, mode_j, slope, prod_hi, prod_lo):
@@ -80,7 +81,7 @@
             parity = 1 - zl if other else zl
 
             def piece_of(zh, piece):
-                return got_ref[zh * 5 + piece] if other else mid_ref[zh, piece]
+                return got_ref[1 - zl, zh * 5 + piece] if other else mid_ref[zh, piece]
 
             block = left.at[pl.ds(pl.multiple_of(parity * 64, 64), 64)]
             for zh in range(4):
@@ -110,12 +111,12 @@
             def _():
                 for y in range(2):
                     for z in range(8):
-                        data = mid_ref[yh, z] if y == own else got_ref[z]
+                        data = mid_ref[yh, z] if y == own else got_ref[1 - own, z]
                         for xl in range(2):
                             row = z * 8 + xl * 4 + y * 2
                             mode_j[row : row + 2, :] = data[2 * xl : 2 * xl + 2, :]
                     for q in range(4):
-                        data = mid_ref[q, 8] if y == own else got_ref[8 + q]
+                        data = mid_ref[q, 8] if y == own else got_ref[1 - own, 8 + q]
                         for xl in range(2):
                             row = xl * 16 + (2 * q + y) * 2
                             slope[row : row + 2, :] = data[2 * xl : 2 * xl + 2, :]
@@ -188,9 +189,9 @@
                 for parity in range(2):
                     second.append([device(xh, 0, parity + 2 * n, xl, kept) for n in range(4)])
                     second.append([device(xh, 1, kept, xl, parity + 2 * n) for n in range(4)])
-                for n in range(8):
-                    third.append((device(xh, 0, n, xl, kept), device(xh, 0, n ^ 1, xl, kept)))
-                    third.append((device(xh, 1, kept, xl, n), device(xh, 1, kept, xl, n ^ 1)))
+                for n in range(0, 8, 2):
+                    third.append([device(xh, 0, n, xl, kept), device(xh, 0, n + 1, xl, kept)])
+                    third.append([device(xh, 1, kept, xl, n), device(xh, 1, kept, xl, n + 1)])
     return first, second, third
 
 
@@ -224,12 +225,12 @@
     mid = on_chip(lax.all_to_all(picked, AXES, 0, 0, axis_index_groups=second, tiled=True))
     packed = pl.pallas_call(
         pack_kernel,
-        out_shape=pltpu.VMEM((20, 4, half), f32),
+        out_shape=pltpu.VMEM((2, 20, 4, half), f32),
         in_specs=[VMEM],
         out_specs=VMEM,
         compiler_params=room(8),
     )(mid)
-    got = on_chip(lax.ppermute(packed, AXES, third))
+    got = on_chip(lax.all_to_all(packed, AXES, 0, 0, axis_index_groups=third, tiled=True))
     piece = pltpu.VMEM((4, 8, 2, 2, 8, 128), f32)
     keep, send = pl.pallas_call(
         tensor_kernel,

time: 102 us -> 103 us (level)
  blocking collectives: 81.4 us -> 93 us
  waiting for transfers between devices: 10.1 us -> 1.88 us
  starting transfers between devices: 4.4 us -> 1.92 us
    all_to_all x0 -> x1, blocking collectives: none -> 11.5 us  [per_device(): lax.all_to_all(packed, AXES, 0, 0, axis_index_groups=third, tiled=True)]
    ppermute x1 -> x0, waiting for transfers between devices: 8.23 us -> none  [per_device(): got = on_chip(lax.ppermute(packed, AXES, third))]
    ppermute x1 -> x0, starting transfers between devices: 2.48 us -> none  [per_device(): got = on_chip(lax.ppermute(packed, AXES, third))]
  transfers between devices with their start and end apart: 2 -> 1, of which waited for: 2 -> 1; matrix products, arithmetic and copies ran while one was open for 0% -> 0% of each run, Pallas kernels for 0% -> 0%
where the time goes in v9:
time: 103 us
  blocking collectives  93 us (90%)
  Pallas kernels  5.7 us (6%)
  starting transfers between devices  1.92 us (2%)
  waiting for transfers between devices  1.88 us (2%)
    all_to_all x1, blocking collectives, per_device(): lax.all_to_all(picked, AXES, 0, 0, axis_index_groups=second, tiled=True)  33.3 us
    all_to_all x1, blocking collectives, per_device(): lax.all_to_all(pair.reshape(128, 8, 128), ('xh', 'zh', 'zl', 'xl', 'yl'),...  30.2 us
    all_to_all x1, blocking collectives, per_device(): lax.all_to_all(spread.reshape(16, 4, half), AXES, 0, 0, axis_index_groups...  18 us
    all_to_all x1, blocking collectives, per_device(): lax.all_to_all(packed, AXES, 0, 0, axis_index_groups=third, tiled=True)  11.5 us
    pallas_call x1, Pallas kernels, per_device(): pl.pallas_call(tensor_kernel, out_shape=(piece, piece), in_specs=[VMEM, V...  3.91 us
  transfers between devices with their start and end apart: 1, of which 1 were waited for; matrix products, arithmetic and copies ran while one was open for 0% of the time, Pallas kernels for 0%

profile of v9, /device:TPU:4, one launch (start us, length us, event | category | flops | bytes accessed | tf_op | source)
XLA Modules:
  0.0 102.6 jit_solution(18065322189065448375)
XLA Ops:
  0.0 0.9 shard_map.28
  0.9 18.0 %all_to_all.20 = f32[16,4,1536]{2,1,0:T(4,128)S(1)} all-to-all(f32[16,4,1536]{2,1,0:T(4,128)S(1)} %bitcast.9), channel_id=1, replica_groups={{0,1,2,3,4,5,6,7,8,9,10,11,12,13,14,15},{128,144,160,176,192,208,224,24..., dimensions={0} | all-to-all | bytes 786432 | tf_op jit(solution)/shard_map/all_to_all | solution.py:216
  18.8 0.1 shard_map.29
  19.0 33.3 %all_to_all.21.mid_ref = f32[4,9,4,1536]{3,2,1,0:T(4,128)S(1)} all-to-all(f32[4,9,4,1536]{3,2,1,0:T(4,128)S(1)} %shard_map.29), channel_id=1, replica_groups={{0,32,64,96},{128,130,132,134},{16,48,80,112},{129,131,133,135},{8,40,7..., dimensions={0} | all-to-all | bytes 1769472 | tf_op jit(solution)/shard_map/all_to_all | solution.py:225
  52.3 11.5 %all_to_all.22.got_ref = f32[2,20,4,1536]{3,2,1,0:T(4,128)S(1)} all-to-all(f32[2,20,4,1536]{3,2,1,0:T(4,128)S(1)} %shard_map.30), channel_id=1, replica_groups={{0,16},{128,129},{32,48},{130,131},{64,80},{132,133},{96,112},{134,135}..., dimensions={0} | all-to-all | bytes 1966080 | tf_op jit(solution)/shard_map/all_to_all | solution.py:233
  63.8 3.9 %shard_map.31 = (f32[4,8,2,2,8,128]{5,4,3,2,1,0:T(8,128)S(1)}, f32[4,8,2,2,8,128]{5,4,3,2,1,0:T(8,128)S(1)}) custom-call(f32[2,8,4,1536]{3,2,1,0:T(4,128)S(1)} %bitcast.7, f32[4,9,4,1536]{3,2,1,0:T(4,128)S(1)} %all_to_all.21.mid_ref, f32[2,20,4,1536]{3,2,1,0:T(4,128)S(1)} %all_to_all.22.got_ref), custom_call_target="tpu_custom_call" | custom-call | tf_op jit(solution)/shard_map/pallas_call | solution.py:235
  67.7 1.9 %collective-permute-start = (f32[4,8,2,2,8,128]{5,4,3,2,1,0:T(8,128)S(1)}, f32[4,8,2,2,8,128]{5,4,3,2,1,0:T(8,128)S(1)}, u32[]{:S(2)}, u32[]{:S(2)}) collective-permute-start(f32[4,8,2,2,8,128]{5,4,3,2,1,0:T(8,128)S(1)} %get-tuple-element.8), channel_id=1, source_target_pairs={{0,128},{128,0},{1,129},{129,1},{2,130},{130,2},{3,131},{131,3},{4... | collective-permute-start | bytes 1572872 | tf_op jit(solution)/shard_map/ppermute | solution.py:250
  69.7 1.9 %collective-permute-done = f32[4,8,2,2,8,128]{5,4,3,2,1,0:T(8,128)S(1)} collective-permute-done((f32[4,8,2,2,8,128]{5,4,3,2,1,0:T(8,128)S(1)}, f32[4,8,2,2,8,128]{5,4,3,2,1,0:T(8,128)S(1)}, u32[]{:S(2)}, u32[]{:S(2)}) %collective-permute-start) | collective-permute-done | bytes 524320 | tf_op jit(solution)/shard_map/ppermute | solution.py:250
  71.5 0.1 add.3
  71.6 30.2 %all_to_all.23 = f32[128,8,128]{2,1,0:T(8,128)S(1)} all-to-all(f32[128,8,128]{2,1,0:T(8,128)S(1)} %bitcast.10), channel_id=1, replica_groups=mesh['xh'=4,'core'=2,'zh'=4,'zl'=2,'xl'=2,'yh'=4,'yl'=2] {'xh','zh','zl'..., dimensions={0} | all-to-all | bytes 1048576 | tf_op jit(solution)/shard_map/all_to_all | solution.py:251
  101.8 0.8 shard_map.32
  (1 shorter events, 0.0 us)
Async XLA Ops:
  67.7 3.8 %collective-permute-start = (f32[4,8,2,2,8,128]{5,4,3,2,1,0:T(8,128)S(1)}, f32[4,8,2,2,8,128]{5,4,3,2,1,0:T(8,128)S(1)}, u32[]{:S(2)}, u32[]{:S(2)}) collective-permute-start(f32[4,8,2,2,8,128]{5,4,3,2,1,0:T(8,128)S(1)} %get-tuple-element.8), channel_id=1, source_target_pairs={{0,128},{128,0},{1,129},{129,1},{2,130},{130,2},{3,131},{131,3},{4... | collective-permute-start | bytes 1572872 | tf_op jit(solution)/shard_map/ppermute | solution.py:250
